TPU v7x, 32 devices: a whole 2x2x4 slice. The times are simulated.
32 devices in a mesh: fsdp: 4 (over x, core), ctx: 4 (over z), tensor: 2 (over y).
Axes of the slice: x: 2, y: 2, z: 4, core: 2. Of those that a mesh axis runs over, the one named last changes fastest.
Arguments:
- block_input: bfloat16 [4096, 2048], P(('fsdp', 'ctx')), may hold values from -6 to 6
- seq_lengths: int32 [4, 3], P('fsdp'), may hold values from 1 to 512, 1024 in all within a row
- attn_gain: bfloat16 [2048], P('fsdp'), may hold values from 0.5 to 1.5
- w_query: bfloat16 [2048, 2048], P('fsdp', 'tensor'), as said below
- w_key: bfloat16 [2048, 512], P('fsdp', 'tensor'), as said below
- w_value: bfloat16 [2048, 512], P('fsdp', 'tensor'), may hold values from -0.125 to 0.125
- w_output: bfloat16 [2048, 2048], P('tensor', 'fsdp'), may hold values from -2 to 2
- mlp_gain: bfloat16 [2048], P('fsdp'), may hold values from 0.5 to 1.5
- w_gate: bfloat16 [2048, 8192], P('fsdp', 'tensor'), may hold values from -0.125 to 0.125
- w_up: bfloat16 [2048, 8192], P('fsdp', 'tensor'), may hold values from -0.125 to 0.125
- w_down: bfloat16 [8192, 2048], P('tensor', 'fsdp'), may hold values from -0.0625 to 0.0625
- cotangent: bfloat16 [4096, 2048], P(('fsdp', 'ctx')), may hold values from -6 to 6
Outputs:
- block_output: bfloat16 [4096, 2048], P(('fsdp', 'ctx'))
- input_grad: float32 [4096, 2048], P(('fsdp', 'ctx'))
- attn_gain_grad: float32 [2048], P('fsdp')
- query_grad: float32 [2048, 2048], P('fsdp', 'tensor')
- key_grad: float32 [2048, 512], P('fsdp', 'tensor')
- value_grad: float32 [2048, 512], P('fsdp', 'tensor')
- output_grad: float32 [2048, 2048], P('tensor', 'fsdp')
- mlp_gain_grad: float32 [2048], P('fsdp')
- gate_grad: float32 [2048, 8192], P('fsdp', 'tensor')
- up_grad: float32 [2048, 8192], P('fsdp', 'tensor')
- down_grad: float32 [8192, 2048], P('tensor', 'fsdp')
Inputs may be any that keep to these rules, and one draw needn't show every extreme that they name: `seq_lengths`: each row sums to 1024, and its largest entry is exactly 512. `w_query`: a projection matrix. `w_key`: a projection matrix.
All inputs are finite; a program needn't handle non-finite values.
Results may differ from a plain program's by a relative error of at most 0.02.
Values may be sent and summed in bfloat16 or wider, within the bound.
No kernel may reach another device: no remote copies, remote signals or barrier semaphores. Data moves between devices by JAX's collectives and lax.ppermute only.
A program may use at most 320 MiB of HBM per device.

v0:
```python
import math

import jax
import jax.numpy as jnp
from jax import lax
from jax.sharding import PartitionSpec as P


HD = 64
MAXLEN = 512

eps_norm = 1e-05
rope_base = 500000.0

BF = jnp.bfloat16
F32 = jnp.float32


def layout(lengths, token_index):
    seq_ends = jnp.cumsum(lengths, axis=1)
    passed = (token_index[None, :, None] >= seq_ends[:, None, :]).astype(jnp.int32)
    segment = jnp.sum(passed, axis=2)
    seq_start = jnp.sum(passed * lengths[:, None, :], axis=2)
    return segment, token_index[None, :] - seq_start


def rope_tables(position):
    half_width = HD // 2
    frequency = rope_base ** (-jnp.arange(half_width, dtype=F32) / half_width)
    angles = position.astype(F32)[:, None] * frequency[None, :]
    return jnp.cos(angles), jnp.sin(angles)


def rotate(vectors, cosine_table, sine_table, direction):
    half_width = HD // 2
    first_half = vectors[..., :half_width]
    second = vectors[..., half_width:]
    cos_rows = cosine_table[:, None, :]
    sin_rows = direction * sine_table[:, None, :]
    return jnp.concatenate(
        [first_half * cos_rows - second * sin_rows, second * cos_rows + first_half * sin_rows],
        axis=-1,
    )


def norm_forward(rows_wide):
    inv_rms = lax.rsqrt(jnp.mean(rows_wide * rows_wide, axis=-1, keepdims=True) + eps_norm)
    return rows_wide * inv_rms, inv_rms


def norm_backward(delta_rows, unit_rows, inv_rms, gain_wide):
    scaled = gain_wide[None, :] * delta_rows
    gain_term = jnp.sum(delta_rows * unit_rows, axis=0)
    back_term = inv_rms * (
        scaled - unit_rows * jnp.mean(scaled * unit_rows, axis=-1, keepdims=True)
    )
    return gain_term, back_term


def dot(a, b):
    return jnp.dot(a, b, preferred_element_type=F32)


def dot_t(a, b):
    return lax.dot_general(a, b, (((0,), (0,)), ((), ())), preferred_element_type=F32)


def dot_bt(a, b):
    return lax.dot_general(a, b, (((1,), (1,)), ((), ())), preferred_element_type=F32)


def after(value, *deps):
    return lax.optimization_barrier((value,) + deps)[0] if deps else value


def body(
    block_input,
    seq_lengths,
    attn_gain,
    w_query,
    w_key,
    w_value,
    w_output,
    mlp_gain,
    w_gate,
    w_up,
    w_down,
    cotangent,
):
    rows, _ = block_input.shape
    n_fsdp, n_ctx, n_ten = (lax.axis_size(a) for a in ("fsdp", "ctx", "tensor"))
    heads_local = w_query.shape[1] // HD
    kv_local = w_key.shape[1] // HD
    tp = math.gcd(n_fsdp, kv_local)
    n_out = n_fsdp // tp
    hq, hk = heads_local // tp, kv_local // tp
    share = hq // hk
    ff_part = w_gate.shape[1] // tp
    d_blk = w_query.shape[0]
    score_scale = 1.0 / math.sqrt(HD)
    i = lax.axis_index("fsdp")
    j = i % tp
    z = lax.axis_index("ctx")
    outer_groups = [[o * tp + jj for o in range(n_out)] for jj in range(tp)]
    bits = []
    b = tp // 2
    while b:
        bits.append(b)
        b //= 2

    lanes = {}

    def send(lane, v, axis, perm, depth=1):
        line = lanes.setdefault(lane, []) if lane is not None else []
        held = line[-depth] if len(line) >= depth else ()
        out = lax.ppermute(after(v, *held), axis, perm)
        line.append((out,))
        return out

    def swap(v, r, lane=None):
        return send(lane if r > 1 else None, v, "fsdp", [(s, s ^ r) for s in range(n_fsdp)])

    def shift(v, s):
        pairs = [(k, k + s) for k in range(n_ctx) if 0 <= k + s < n_ctx]
        return send(None, v, "ctx", pairs)

    def gather_rows(v, lane=None):
        for bit in bits:
            v = jnp.concatenate([v, swap(v, bit, lane)], axis=0)
        return v

    def ten_sum(acc):
        low = acc.astype(BF)
        if n_ten == 1:
            return low.astype(F32)
        if n_ten == 2:
            other = send(None, low, "tensor", [(0, 1), (1, 0)])
            return low.astype(F32) + other.astype(F32)
        return lax.psum(low, "tensor").astype(F32)

    def reduce_rows(pairs, mult, lane=None):
        total = tp * rows
        half = total // 2 if tp > 1 else total
        own = sum(mult(a[:half], w) for a, w in pairs)
        if tp > 1:
            part = sum(mult(a[half:], w) for a, w in pairs).astype(BF)
            own = own + swap(part, bits[-1]).astype(F32)
        for bit in reversed(bits[:-1]):
            half //= 2
            own = own[:half] + swap(own[half:].astype(BF), bit, lane).astype(F32)
        return ten_sum(own)

    def place(buffer, value, start, axis):
        starts = [0] * buffer.ndim
        starts[axis] = start
        return lax.dynamic_update_slice(buffer, value, starts)

    def fetch_near(piece, axis, name):
        got = [(piece(j), j)]
        if tp == 4 and n_ctx % 2 == 0:
            odd = z % 2
            perm = [
                (s * n_ctx + k, (s ^ (2 + k % 2)) * n_ctx + k)
                for s in range(n_fsdp)
                for k in range(n_ctx)
            ]
            far = send(None, piece(j ^ (2 + odd)), ("fsdp", "ctx"), perm)
            got.append((far, j ^ (2 + odd)))
            got.append((swap(piece(j ^ 1), 1), j ^ 1))
        else:
            got += [(swap(piece(j ^ r), r), j ^ r) for r in range(1, tp)]
        return got, axis, name

    def fetch_far(state):
        got, axis, _ = state
        if len(got) < tp:
            value, k = got[1]
            value = send(None, value, "ctx", [(a, a ^ 1) for a in range(n_ctx)])
            got = got + [(value, k ^ 1)]
        size = got[0][0].shape[axis]
        shape = list(got[0][0].shape)
        shape[axis] = tp * size
        full = jnp.zeros(shape, BF)
        for value, k in got:
            full = place(full, value, k * size, axis)
        if n_out > 1:
            full = lax.all_gather(full, "fsdp", axis=axis, tiled=True, axis_index_groups=outer_groups)
        return full

    def cols(w, k, size):
        return lax.dynamic_slice_in_dim(w, k * size, size, axis=1)

    def take_rows(w, k, size):
        return lax.dynamic_slice_in_dim(w, k * size, size, axis=0)

    gains = jnp.stack([attn_gain, mlp_gain])
    gain_all = place(jnp.zeros((2, tp * d_blk), BF), gains, j * d_blk, 1)
    for r in range(1, tp):
        gain_all = place(gain_all, swap(gains, r), (j ^ r) * d_blk, 1)
    if n_out > 1:
        gain_all = lax.all_gather(gain_all, "fsdp", axis=1, tiled=True, axis_index_groups=outer_groups)
    gain_one = gain_all[0].astype(F32)
    gain_two = gain_all[1].astype(F32)
    lengths = seq_lengths
    for bit in bits:
        lengths = jnp.concatenate([lengths, swap(lengths, bit)], axis=0)

    qkv_state = fetch_near(
        lambda k: jnp.concatenate(
            [cols(w_query, k, hq * HD), cols(w_key, k, hk * HD), cols(w_value, k, hk * HD)], axis=1
        ),
        0,
        "wqkv",
    )
    input_wide = block_input.astype(F32)
    unit_one, rstd_one = norm_forward(input_wide)
    own_normed = (unit_one * gain_one[None, :]).astype(BF)
    normed_one = gather_rows(own_normed)
    qkv_full = fetch_far(qkv_state)
    half = ff_part // 2
    out_full = fetch_far(fetch_near(lambda k: take_rows(w_output, k, hq * HD), 1, "wo"))
    gate_full = fetch_far(fetch_near(lambda k: cols(w_gate, k, ff_part), 0, "wg"))
    up_full = fetch_far(fetch_near(lambda k: cols(w_up, k, ff_part), 0, "wu"))
    down_full = jnp.concatenate(
        [
            fetch_far(
                fetch_near(
                    lambda k: lax.dynamic_slice_in_dim(w_down, k * ff_part + at, half, axis=0), 1, name
                )
            )
            for at, name in ((0, "wl"), (half, "wh"))
        ],
        axis=0,
    )

    qkv = dot(normed_one, qkv_full)
    local_index = z * rows + jnp.arange(rows, dtype=jnp.int32)
    q_seg, q_pos = layout(lengths, local_index)
    cosine_table, sine_table = rope_tables(q_pos.reshape(tp * rows))
    q_cols, k_cols = hq * HD, hk * HD
    query_rot = rotate(
        qkv[:, :q_cols].reshape(tp * rows, hq, HD), cosine_table, sine_table, 1.0
    ).astype(BF)
    key_rot = rotate(
        qkv[:, q_cols : q_cols + k_cols].reshape(tp * rows, hk, HD), cosine_table, sine_table, 1.0
    ).astype(BF)
    value_rows = qkv[:, q_cols + k_cols :].astype(BF)

    reach = min(-(-(MAXLEN - 1) // rows), n_ctx - 1)
    kv_own = jnp.concatenate([key_rot.reshape(tp * rows, k_cols), value_rows], axis=1)
    kv_blocks = [kv_own] + [shift(kv_own, s) for s in range(1, reach + 1)]
    kv_all = jnp.concatenate(
        [v.reshape(tp, 1, rows, 2, hk, HD) for v in kv_blocks], axis=1
    ).reshape(tp, (reach + 1) * rows, 2, hk, HD)
    key_index = jnp.concatenate(
        [(z - s) * rows + jnp.arange(rows, dtype=jnp.int32) for s in range(reach + 1)]
    )
    k_seg, _ = layout(lengths, key_index)
    allowed = (
        (q_seg[:, :, None] == k_seg[:, None, :])
        & (key_index[None, None, :] <= local_index[None, :, None])
        & (key_index[None, None, :] >= 0)
    )[:, None, None]
    q_h = query_rot.reshape(tp, rows, hk, share, HD).transpose(0, 2, 3, 1, 4)
    k_h = kv_all[:, :, 0].transpose(0, 2, 1, 3)
    v_h = kv_all[:, :, 1].transpose(0, 2, 1, 3)

    scores = jnp.einsum("bgrtd,bgsd->bgrts", q_h, k_h, preferred_element_type=F32) * score_scale
    masked = jnp.where(allowed, scores, -1e30)
    row_max = jnp.max(masked, axis=-1, keepdims=True)
    exp_total = jnp.sum(jnp.where(allowed, jnp.exp(masked - row_max), 0.0), axis=-1, keepdims=True)
    log_total = row_max + jnp.log(exp_total)
    prob = jnp.where(allowed, jnp.exp(masked - log_total), 0.0)
    prob_low = prob.astype(BF)
    attended = jnp.einsum("bgrts,bgsd->bgrtd", prob_low, v_h, preferred_element_type=F32).astype(BF)
    attended_rows = attended.transpose(0, 3, 1, 2, 4).reshape(tp * rows, hq * HD)
    residual = input_wide + reduce_rows([(attended_rows, out_full)], dot)

    cot_all = gather_rows(cotangent)
    unit_two, rstd_two = norm_forward(residual)
    normed_two = gather_rows((unit_two * gain_two[None, :]).astype(BF))
    gate_pre = dot(normed_two, gate_full)
    up_pre = dot(normed_two, up_full)
    sigmoid_gate = jax.nn.sigmoid(gate_pre)
    silu_gate = gate_pre * sigmoid_gate
    activation = (silu_gate * up_pre).astype(BF)
    act_delta = dot_bt(cot_all, down_full)
    silu_slope = sigmoid_gate * (1.0 + gate_pre * (1.0 - sigmoid_gate))
    gate_delta = (act_delta * up_pre * silu_slope).astype(BF)
    up_delta = (act_delta * silu_gate).astype(BF)

    mid = n_ctx // 2

    def ctx_total(part):
        acc = part
        for h in range(mid - 1):
            pairs = [(h, h + 1), (n_ctx - 1 - h, n_ctx - 2 - h)]
            come = send(("in", h), acc, "ctx", pairs, 2)
            acc = (part.astype(F32) + come.astype(F32)).astype(BF)
        come = send("mid", acc, "ctx", [(mid - 1, mid), (mid, mid - 1)], 2)
        value = (acc.astype(F32) + come.astype(F32)).astype(BF)
        for h in reversed(range(mid - 1)):
            pairs = [(h + 1, h), (n_ctx - 2 - h, n_ctx - 1 - h)]
            come = send(("out", h), value, "ctx", pairs, 2)
            value = jnp.where((z == h) | (z == n_ctx - 1 - h), come, value)
        return value

    def exchange(piece, lane):
        line = lanes.setdefault(lane, []) if lane is not None else []
        held, out = (line[-1] if line else ()), [(j, piece(j))]
        for r in range(1, tp):
            out.append((j ^ r, swap(after(piece(j ^ r), *(held if r > 1 else ())), r)))
        line.append(tuple(value for _, value in out[2:]))
        return out

    def finish_rows(view, widths):
        _, b, c = view.shape
        if n_out > 1:
            view = lax.psum_scatter(
                view.reshape(n_out, tp, b, c), "fsdp", scatter_dimension=0, axis_index_groups=outer_groups
            )
        got = exchange(lambda k: lax.dynamic_slice_in_dim(view, k, 1, axis=0)[0], "x")
        mine = jnp.zeros((b, tp * c), BF)
        base = low = 0
        for w in widths:
            for k, value in got:
                mine = lax.dynamic_update_slice(mine, value[:, low : low + w], (0, base + k * w))
            base, low = base + tp * w, low + w
        return mine

    def finish_cols(part):
        b = part.shape[0]
        if n_out > 1:
            part = lax.psum_scatter(
                part.reshape(b, n_out, tp * d_blk), "fsdp", scatter_dimension=1, axis_index_groups=outer_groups
            )
        got = exchange(lambda k: cols(part, k, d_blk), "x")
        mine = jnp.zeros((tp, b, d_blk), BF)
        for k, value in got:
            mine = lax.dynamic_update_slice(mine, value[None], (k, 0, 0))
        return mine

    def grad_cols(left, right, n, chunks):
        b = left.shape[1] // chunks
        return finish_cols(dot_t(left[:, n * b : (n + 1) * b], right).astype(BF))

    def grad_rows(part, widths, n, chunks):
        b = d_blk // chunks
        return finish_rows(part.reshape(n_fsdp, chunks, b, part.shape[1])[:, n], widths)

    def join_cols(done):
        full = jnp.stack([v.astype(F32) for v in done], axis=1)
        return full.reshape(-1, d_blk)

    def join_rows(done):
        return jnp.concatenate([v.astype(F32) for v in done], axis=0)

    up_part = dot_t(normed_two, up_delta).astype(BF)
    gate_part = dot_t(normed_two, gate_delta).astype(BF)
    down_low_grad = ctx_total(grad_cols(activation, cot_all, 0, 2))
    down_high_grad = ctx_total(grad_cols(activation, cot_all, 1, 2))
    normed_two_delta = reduce_rows([(gate_delta, gate_full), (up_delta, up_full)], dot_bt, "x")
    gain_two_term, residual_back = norm_backward(normed_two_delta, unit_two, rstd_two, gain_two)
    residual_delta = cotangent.astype(F32) + residual_back
    up_low_grad = ctx_total(grad_rows(up_part, (ff_part,), 0, 2))
    residual_low = gather_rows(residual_delta.astype(BF), "x")
    up_high_grad = ctx_total(grad_rows(up_part, (ff_part,), 1, 2))
    gate_low_grad = ctx_total(grad_rows(gate_part, (ff_part,), 0, 2))
    output_grad = ctx_total(grad_cols(attended_rows, residual_low, 0, 1))
    gate_high_grad = ctx_total(grad_rows(gate_part, (ff_part,), 1, 2))

    attended_delta = dot_bt(residual_low, out_full).astype(BF)
    delta_h = attended_delta.reshape(tp, rows, hk, share, HD).transpose(0, 2, 3, 1, 4)
    inner_rows = jnp.sum(attended.astype(F32) * delta_h.astype(F32), axis=-1, keepdims=True)
    prob_delta = jnp.einsum("bgrtd,bgsd->bgrts", delta_h, v_h, preferred_element_type=F32)
    score_delta = (prob * (prob_delta - inner_rows) * score_scale).astype(BF)
    query_back = jnp.einsum("bgrts,bgsd->bgrtd", score_delta, k_h, preferred_element_type=F32)
    key_back = jnp.einsum("bgrts,bgrtd->bgsd", score_delta, q_h, preferred_element_type=F32)
    value_back = jnp.einsum("bgrts,bgrtd->bgsd", prob_low, delta_h, preferred_element_type=F32)

    def to_blocks(v):
        v = v.transpose(0, 2, 1, 3).reshape(tp, reach + 1, rows, k_cols)
        return [v[:, s].reshape(tp * rows, k_cols) for s in range(reach + 1)]

    kv_back = [
        jnp.concatenate([kb, vb], axis=1) for kb, vb in zip(to_blocks(key_back), to_blocks(value_back))
    ]
    kv_sum = kv_back[0]
    for s in range(1, reach + 1):
        kv_sum = kv_sum + shift(kv_back[s].astype(BF), -s).astype(F32)
    query_delta = rotate(
        query_back.transpose(0, 3, 1, 2, 4).reshape(tp * rows, hq, HD), cosine_table, sine_table, -1.0
    ).reshape(tp * rows, q_cols)
    key_delta = rotate(
        kv_sum[:, :k_cols].reshape(tp * rows, hk, HD), cosine_table, sine_table, -1.0
    ).reshape(tp * rows, k_cols)
    qkv_delta = jnp.concatenate([query_delta, key_delta, kv_sum[:, k_cols:]], axis=1).astype(BF)
    qkv_part = dot_t(normed_one, qkv_delta).astype(BF)
    qkv_out = join_rows(
        [ctx_total(grad_rows(qkv_part, (q_cols, k_cols, k_cols), n, 2)) for n in range(2)]
    )
    normed_one_delta = reduce_rows([(qkv_delta, qkv_full)], dot_bt, "x")
    block_output = (residual + reduce_rows([(activation, down_full)], dot, "x")).astype(BF)
    gain_one_term, input_back = norm_backward(normed_one_delta, unit_one, rstd_one, gain_one)
    input_grad = residual_delta + input_back

    terms = jnp.stack([gain_one_term, gain_two_term])
    if n_out > 1:
        terms = lax.psum_scatter(
            terms.reshape(2, n_out, tp * d_blk), "fsdp", scatter_dimension=1, axis_index_groups=outer_groups
        )
    got = exchange(lambda k: cols(terms, k, d_blk), None)
    gain_sum = sum(value for _, value in got)
    step = 1
    while step < n_ctx:
        gain_sum = gain_sum + lax.ppermute(gain_sum, "ctx", [(k, k ^ step) for k in range(n_ctx)])
        step *= 2
    gain_grads = gain_sum

    q_all, k_all = tp * q_cols, tp * k_cols
    return (
        block_output,
        input_grad,
        gain_grads[0],
        qkv_out[:, :q_all],
        qkv_out[:, q_all : q_all + k_all],
        qkv_out[:, q_all + k_all :],
        join_cols([output_grad]),
        gain_grads[1],
        join_rows([gate_low_grad, gate_high_grad]),
        join_rows([up_low_grad, up_high_grad]),
        join_cols([down_low_grad, down_high_grad]),
    )


def solution(mesh):
    in_specs = (
        P(("fsdp", "ctx"), None),
        P("fsdp", None),
        P("fsdp"),
        P("fsdp", "tensor"),
        P("fsdp", "tensor"),
        P("fsdp", "tensor"),
        P("tensor", "fsdp"),
        P("fsdp"),
        P("fsdp", "tensor"),
        P("fsdp", "tensor"),
        P("tensor", "fsdp"),
        P(("fsdp", "ctx"), None),
    )
    out_specs = (
        P(("fsdp", "ctx"), None),
        P(("fsdp", "ctx"), None),
        P("fsdp"),
        P("fsdp", "tensor"),
        P("fsdp", "tensor"),
        P("fsdp", "tensor"),
        P("tensor", "fsdp"),
        P("fsdp"),
        P("fsdp", "tensor"),
        P("fsdp", "tensor"),
        P("tensor", "fsdp"),
    )

    return jax.shard_map(body, mesh=mesh, in_specs=in_specs, out_specs=out_specs, check_vma=False)
```

profile of v0, /device:TPU:0, one launch (start us, length us, event | category | flops | bytes accessed | tf_op | source)
XLA Modules:
  0.0 1099.1 jit_solution(14111528774380275819)
XLA Ops:
  18.6 17.3 %collective-permute-done.5 = bf16[256,2048]{1,0:T(8,128)(2,1)} collective-permute-done((bf16[256,2048]{1,0:T(8,128)(2,1)}, bf16[256,2048]{1,0:T(8,128)(2,1)}, u32[]{:S(2)}, u32[]{:S(2)}) %collective-permute-start.5) | collective-permute-done | bytes 1048608 | tf_op jit(solution)/shard_map/ppermute | solution.py:116
  39.3 10.0 collective-permute-done
  60.7 10.4 collective-permute-done.9
  123.4 23.7 %collective-permute-done.16 = bf16[256,2048]{1,0:T(8,128)(2,1)S(1)} collective-permute-done((bf16[256,2048]{1,0:T(8,128)(2,1)S(1)}, bf16[256,2048]{1,0:T(8,128)(2,1)S(1)}, u32[]{:S(2)}, u32[]{:S(2)}) %collective-permute-start.16) | collective-permute-done | bytes 1048608 | tf_op jit(solution)/shard_map/ppermute | solution.py:116
  157.2 14.7 %collective-permute-done.17 = bf16[256,2048]{1,0:T(8,128)(2,1)} collective-permute-done((bf16[256,2048]{1,0:T(8,128)(2,1)S(1)}, bf16[256,2048]{1,0:T(8,128)(2,1)}, u32[]{:S(2)}, u32[]{:S(2)}) %collective-permute-start.17) | collective-permute-done | bytes 1048608 | tf_op jit(solution)/shard_map/ppermute | solution.py:116
  188.1 9.7 collective-permute-done.26
  210.4 9.9 collective-permute-done.18
  221.7 21.0 %collective-permute-done.23 = bf16[512,1024]{1,0:T(8,128)(2,1)} collective-permute-done((bf16[512,1024]{1,0:T(8,128)(2,1)}, bf16[512,1024]{1,0:T(8,128)(2,1)}, u32[]{:S(2)}, u32[]{:S(2)}) %collective-permute-start.23) | collective-permute-done | bytes 1048608 | tf_op jit(solution)/shard_map/ppermute | solution.py:116
  250.0 13.3 %collective-permute-done.20 = bf16[512,1024]{1,0:T(8,128)(2,1)} collective-permute-done((bf16[512,1024]{1,0:T(8,128)(2,1)}, bf16[512,1024]{1,0:T(8,128)(2,1)}, u32[]{:S(2)}, u32[]{:S(2)}) %collective-permute-start.20) | collective-permute-done | bytes 1048608 | tf_op jit(solution)/shard_map/ppermute | solution.py:116
  282.2 15.8 %collective-permute-done.25 = bf16[512,1024]{1,0:T(8,128)(2,1)S(1)} collective-permute-done((bf16[512,1024]{1,0:T(8,128)(2,1)}, bf16[512,1024]{1,0:T(8,128)(2,1)S(1)}, u32[]{:S(2)}, u32[]{:S(2)}) %collective-permute-start.25) | collective-permute-done | bytes 1048608 | tf_op jit(solution)/shard_map/ppermute | solution.py:116
  298.2 21.7 %collective-permute-done.22 = bf16[512,1024]{1,0:T(8,128)(2,1)S(1)} collective-permute-done((bf16[512,1024]{1,0:T(8,128)(2,1)}, bf16[512,1024]{1,0:T(8,128)(2,1)S(1)}, u32[]{:S(2)}, u32[]{:S(2)}) %collective-permute-start.22) | collective-permute-done | bytes 1048608 | tf_op jit(solution)/shard_map/ppermute | solution.py:116
  324.0 9.8 fusion.79
  341.9 11.3 %multiply_convert_fusion.2 = (bf16[1024,1024]{1,0:T(8,128)(2,1)}, bf16[1024,1024]{1,0:T(8,128)(2,1)}, bf16[1024,1024]{1,0:T(8,128)(2,1)}) fusion(f32[1024,1024]{1,0:T(8,128)} %fusion.79, f32[1024,1024]{1,0:T(8,128)} %fusion.78, bf16[1024,2048]{1,0:T(8,128)(2,1)S(1)} %copy-done.63, bf16[512,2048]{1,0:T(8,128)(2,1)S(1)} %constant_dynamic-update-slice_fusion.12, ...), kind=kOutput, calls=%fused_computation.30 | convolution fusion | flops 4319084544 | bytes 23068672 | tf_op jit(solution)/shard_map/dot_general | solution.py:69
  406.9 10.8 collective-permute-done.38
  443.2 10.0 collective-permute-done.40
  455.6 11.7 %collective-permute-done.91 = bf16[4,512,512]{2,1,0:T(8,128)(2,1)S(1)} collective-permute-done((bf16[4,512,512]{2,1,0:T(8,128)(2,1)S(1)}, bf16[4,512,512]{2,1,0:T(8,128)(2,1)S(1)}, u32[]{:S(2)}, u32[]{:S(2)}) %collective-permute-start.91) | collective-permute-done | bytes 2097184 | tf_op jit(solution)/shard_map/ppermute | solution.py:116
  468.0 42.2 %collective-permute-done.74 = bf16[4,512,512]{2,1,0:T(8,128)(2,1)S(1)} collective-permute-done((bf16[4,512,512]{2,1,0:T(8,128)(2,1)S(1)}, bf16[4,512,512]{2,1,0:T(8,128)(2,1)S(1)}, u32[]{:S(2)}, u32[]{:S(2)}) %collective-permute-start.74) | collective-permute-done | bytes 2097184 | tf_op jit(solution)/shard_map/ppermute | solution.py:116
  512.6 10.0 collective-permute-start.92
  535.4 15.2 %collective-permute-done.44 = bf16[256,2048]{1,0:T(8,128)(2,1)S(1)} collective-permute-done((bf16[256,2048]{1,0:T(8,128)(2,1)S(1)}, bf16[256,2048]{1,0:T(8,128)(2,1)S(1)}, u32[]{:S(2)}, u32[]{:S(2)}) %collective-permute-start.44) | collective-permute-done | bytes 1048608 | tf_op jit(solution)/shard_map/ppermute | solution.py:116
  554.4 11.1 %collective-permute-done.49 = bf16[256,1024]{1,0:T(8,128)(2,1)S(1)} collective-permute-done((bf16[256,1024]{1,0:T(8,128)(2,1)S(1)}, bf16[256,1024]{1,0:T(8,128)(2,1)S(1)}, u32[]{:S(2)}, u32[]{:S(2)}) %collective-permute-start.49) | collective-permute-done | bytes 524320 | tf_op jit(solution)/shard_map/ppermute | solution.py:116
  565.5 8.3 collective-permute-done.50
  591.1 8.6 collective-permute-done.52
  599.8 40.9 %collective-permute-start.75 = (bf16[256,4096]{1,0:T(8,128)(2,1)}, bf16[256,4096]{1,0:T(8,128)(2,1)}, u32[]{:S(2)}, u32[]{:S(2)}) collective-permute-start(bf16[256,4096]{1,0:T(8,128)(2,1)} %constant_dynamic-update-slice_fusion.9), channel_id=1, source_target_pairs={{0,2},{6,4},{1,3},{7,5},{8,10},{14,12},{9,11},{15,13},{16,18},{22,... | collective-permute-start | bytes 6291464 | tf_op jit(solution)/shard_map/ppermute | solution.py:116
  641.8 15.7 %collective-permute-done.82 = bf16[4,512,512]{2,1,0:T(8,128)(2,1)S(1)} collective-permute-done((bf16[4,512,512]{2,1,0:T(8,128)(2,1)S(1)}, bf16[4,512,512]{2,1,0:T(8,128)(2,1)S(1)}, u32[]{:S(2)}, u32[]{:S(2)}) %collective-permute-start.82) | collective-permute-done | bytes 2097184 | tf_op jit(solution)/shard_map/ppermute | solution.py:116
  685.0 8.5 multiply_convert_fusion
  765.3 9.8 collective-permute-done.56
  845.3 37.9 %collective-permute-done.77 = bf16[256,1536]{1,0:T(8,128)(2,1)} collective-permute-done((bf16[256,1536]{1,0:T(8,128)(2,1)}, bf16[256,1536]{1,0:T(8,128)(2,1)}, u32[]{:S(2)}, u32[]{:S(2)}) %collective-permute-start.77) | collective-permute-done | bytes 786464 | tf_op jit(solution)/shard_map/ppermute | solution.py:116
  915.6 16.1 %collective-permute-done.64 = bf16[256,2048]{1,0:T(8,128)(2,1)S(1)} collective-permute-done((bf16[256,2048]{1,0:T(8,128)(2,1)S(1)}, bf16[256,2048]{1,0:T(8,128)(2,1)S(1)}, u32[]{:S(2)}, u32[]{:S(2)}) %collective-permute-start.64) | collective-permute-done | bytes 1048608 | tf_op jit(solution)/shard_map/ppermute | solution.py:116
  941.7 44.8 %collective-permute-done.68 = f32[2,512]{1,0:T(2,128)S(1)} collective-permute-done((f32[2,512]{1,0:T(2,128)S(1)}, f32[2,512]{1,0:T(2,128)S(1)}, u32[]{:S(2)}, u32[]{:S(2)}) %collective-permute-start.68) | collective-permute-done | bytes 4128 | tf_op jit(solution)/shard_map/ppermute | solution.py:416
  1001.4 8.8 collective-permute-done.63
  1023.4 54.7 %collective-permute-done.85 = bf16[256,1536]{1,0:T(8,128)(2,1)S(1)} collective-permute-done((bf16[256,1536]{1,0:T(8,128)(2,1)S(1)}, bf16[256,1536]{1,0:T(8,128)(2,1)S(1)}, u32[]{:S(2)}, u32[]{:S(2)}) %collective-permute-start.85) | collective-permute-done | bytes 786464 | tf_op jit(solution)/shard_map/ppermute | solution.py:116
  1084.3 11.7 %collective-permute-done.105 = bf16[256,1536]{1,0:T(8,128)(2,1)S(1)} collective-permute-done((bf16[256,1536]{1,0:T(8,128)(2,1)S(1)}, bf16[256,1536]{1,0:T(8,128)(2,1)S(1)}, u32[]{:S(2)}, u32[]{:S(2)}) %collective-permute-start.105) | collective-permute-done | bytes 786464 | tf_op jit(solution)/shard_map/ppermute | solution.py:116
  (666 shorter events, 530.2 us)
Async XLA Ops:
  149.0 51.7 %collective-permute-start.33 = (bf16[256,2048]{1,0:T(8,128)(2,1)}, bf16[256,2048]{1,0:T(8,128)(2,1)}, u32[]{:S(2)}, u32[]{:S(2)}) collective-permute-start(bf16[256,2048]{1,0:T(8,128)(2,1)} %param.23), channel_id=1, source_target_pairs={{0,16},{8,24},{16,0},{24,8},{1,17},{9,25},{17,1},{25,9},{2,18},{10... | collective-permute-start | bytes 3145736 | tf_op jit(solution)/shard_map/ppermute | solution.py:116
  186.6 56.2 %collective-permute-start.23 = (bf16[512,1024]{1,0:T(8,128)(2,1)}, bf16[512,1024]{1,0:T(8,128)(2,1)}, u32[]{:S(2)}, u32[]{:S(2)}) collective-permute-start(bf16[512,1024]{1,0:T(8,128)(2,1)} %get-tuple-element.115), channel_id=1, source_target_pairs={{0,16},{2,26},{4,20},{6,30},{8,24},{10,18},{12,28},{14,22},{16,0},... | collective-permute-start | bytes 3145736 | tf_op jit(solution)/shard_map/ppermute | solution.py:116
  188.1 54.7 %collective-permute-start.24 = (bf16[512,1024]{1,0:T(8,128)(2,1)}, bf16[512,1024]{1,0:T(8,128)(2,1)}, u32[]{:S(2)}, u32[]{:S(2)}) collective-permute-start(bf16[512,1024]{1,0:T(8,128)(2,1)} %get-tuple-element.113), channel_id=1, source_target_pairs={{0,8},{8,0},{16,24},{24,16},{1,9},{9,1},{17,25},{25,17},{2,10},{10... | collective-permute-start | bytes 3145736 | tf_op jit(solution)/shard_map/ppermute | solution.py:116
  197.8 65.4 %collective-permute-start.20 = (bf16[512,1024]{1,0:T(8,128)(2,1)}, bf16[512,1024]{1,0:T(8,128)(2,1)}, u32[]{:S(2)}, u32[]{:S(2)}) collective-permute-start(bf16[512,1024]{1,0:T(8,128)(2,1)} %get-tuple-element.112), channel_id=1, source_target_pairs={{0,16},{2,26},{4,20},{6,30},{8,24},{10,18},{12,28},{14,22},{16,0},... | collective-permute-start | bytes 3145736 | tf_op jit(solution)/shard_map/ppermute | solution.py:116
  203.8 63.0 %collective-permute-start.31 = (bf16[512,512]{1,0:T(8,128)(2,1)}, bf16[512,512]{1,0:T(8,128)(2,1)S(1)}, u32[]{:S(2)}, u32[]{:S(2)}) collective-permute-start(bf16[512,512]{1,0:T(8,128)(2,1)} %collective-permute-done.29), channel_id=1, source_target_pairs={{0,2},{2,0},{4,6},{6,4},{1,3},{3,1},{5,7},{7,5},{8,10},{10,8},{12,... | collective-permute-start | bytes 1572872 | tf_op jit(solution)/shard_map/ppermute | solution.py:116
  220.3 100.6 %collective-permute-start.34 = (bf16[512,2048]{1,0:T(8,128)(2,1)S(1)}, bf16[512,2048]{1,0:T(8,128)(2,1)S(1)}, u32[]{:S(2)}, u32[]{:S(2)}) collective-permute-start(bf16[512,2048]{1,0:T(8,128)(2,1)S(1)} %pad_maximum_fusion.7), channel_id=1, source_target_pairs={{0,8},{8,0},{16,24},{24,16},{1,9},{9,1},{17,25},{25,17},{2,10},{10... | collective-permute-start | bytes 6291464 | tf_op jit(solution)/shard_map/ppermute | solution.py:116
  263.3 60.8 %collective-permute-start.19 = (bf16[512,2048]{1,0:T(8,128)(2,1)S(1)}, bf16[512,2048]{1,0:T(8,128)(2,1)S(1)}, u32[]{:S(2)}, u32[]{:S(2)}) collective-permute-start(bf16[512,2048]{1,0:T(8,128)(2,1)S(1)} %pad_maximum_fusion.6), channel_id=1, source_target_pairs={{0,8},{8,0},{16,24},{24,16},{1,9},{9,1},{17,25},{25,17},{2,10},{10... | collective-permute-start | bytes 6291464 | tf_op jit(solution)/shard_map/ppermute | solution.py:116
  372.5 49.0 %collective-permute-start.35 = (bf16[512,2048]{1,0:T(8,128)(2,1)}, bf16[512,2048]{1,0:T(8,128)(2,1)}, u32[]{:S(2)}, u32[]{:S(2)}) collective-permute-start(bf16[512,2048]{1,0:T(8,128)(2,1)} %add_convert_fusion.12), channel_id=1, source_target_pairs={{0,8},{8,0},{16,24},{24,16},{1,9},{9,1},{17,25},{25,17},{2,10},{10... | collective-permute-start | bytes 6291464 | tf_op jit(solution)/shard_map/ppermute | solution.py:116
  417.7 49.6 %collective-permute-start.91 = (bf16[4,512,512]{2,1,0:T(8,128)(2,1)S(1)}, bf16[4,512,512]{2,1,0:T(8,128)(2,1)S(1)}, u32[]{:S(2)}, u32[]{:S(2)}) collective-permute-start(bf16[4,512,512]{2,1,0:T(8,128)(2,1)S(1)} %bitcast_dynamic-update-slice_fusion), channel_id=1, source_target_pairs={{0,2},{6,4},{1,3},{7,5},{8,10},{14,12},{9,11},{15,13},{16,18},{22,... | collective-permute-start | bytes 6291464 | tf_op jit(solution)/shard_map/ppermute | solution.py:116
  429.1 81.1 %collective-permute-start.74 = (bf16[4,512,512]{2,1,0:T(8,128)(2,1)S(1)}, bf16[4,512,512]{2,1,0:T(8,128)(2,1)S(1)}, u32[]{:S(2)}, u32[]{:S(2)}) collective-permute-start(bf16[4,512,512]{2,1,0:T(8,128)(2,1)S(1)} %bitcast_dynamic-update-slice_fusion.7), channel_id=1, source_target_pairs={{0,2},{6,4},{1,3},{7,5},{8,10},{14,12},{9,11},{15,13},{16,18},{22,... | collective-permute-start | bytes 6291464 | tf_op jit(solution)/shard_map/ppermute | solution.py:116
  439.8 88.1 %collective-permute-start.32 = (bf16[512,2048]{1,0:T(8,128)(2,1)S(1)}, bf16[512,2048]{1,0:T(8,128)(2,1)}, u32[]{:S(2)}, u32[]{:S(2)}) collective-permute-start(bf16[512,2048]{1,0:T(8,128)(2,1)S(1)} %convolution_convert_fusion.4), channel_id=1, source_target_pairs={{0,8},{8,0},{16,24},{24,16},{1,9},{9,1},{17,25},{25,17},{2,10},{10... | collective-permute-start | bytes 6291464 | tf_op jit(solution)/shard_map/ppermute | solution.py:116
  453.5 59.1 %collective-permute-start.41 = (bf16[256,2048]{1,0:T(8,128)(2,1)S(1)}, bf16[256,2048]{1,0:T(8,128)(2,1)S(1)}, u32[]{:S(2)}, u32[]{:S(2)}) collective-permute-start(bf16[256,2048]{1,0:T(8,128)(2,1)S(1)} %fusion.15), channel_id=1, source_target_pairs={{0,1},{1,0},{2,3},{3,2},{4,5},{5,4},{6,7},{7,6},{8,9},{9,8},{10,11... | collective-permute-start | bytes 3145736 | tf_op jit(solution)/shard_map/ppermute | solution.py:116
  454.1 56.7 %collective-permute-start.42 = (bf16[256,1024]{1,0:T(8,128)(2,1)S(1)}, bf16[256,1024]{1,0:T(8,128)(2,1)S(1)}, u32[]{:S(2)}, u32[]{:S(2)}) collective-permute-start(bf16[256,1024]{1,0:T(8,128)(2,1)S(1)} %copy-done.56), channel_id=1, source_target_pairs={{0,16},{8,24},{16,0},{24,8},{1,17},{9,25},{17,1},{25,9},{2,18},{10... | collective-permute-start | bytes 1572872 | tf_op jit(solution)/shard_map/ppermute | solution.py:116
  512.6 61.8 %collective-permute-start.92 = (bf16[256,4096]{1,0:T(8,128)(2,1)S(1)}, bf16[256,4096]{1,0:T(8,128)(2,1)S(1)}, u32[]{:S(2)}, u32[]{:S(2)}) collective-permute-start(bf16[256,4096]{1,0:T(8,128)(2,1)S(1)} %constant_dynamic-update-slice_fusion), channel_id=1, source_target_pairs={{0,2},{6,4},{1,3},{7,5},{8,10},{14,12},{9,11},{15,13},{16,18},{22,... | collective-permute-start | bytes 6291464 | tf_op jit(solution)/shard_map/ppermute | solution.py:116
  534.1 107.4 %collective-permute-start.101 = (bf16[4,512,512]{2,1,0:T(8,128)(2,1)S(1)}, bf16[4,512,512]{2,1,0:T(8,128)(2,1)S(1)}, u32[]{:S(2)}, u32[]{:S(2)}) collective-permute-start(bf16[4,512,512]{2,1,0:T(8,128)(2,1)S(1)} %add_convert_fusion), channel_id=1, source_target_pairs={{2,0},{4,6},{3,1},{5,7},{10,8},{12,14},{11,9},{13,15},{18,16},{20,... | collective-permute-start | bytes 6291464 | tf_op jit(solution)/shard_map/ppermute | solution.py:116
  552.7 104.8 %collective-permute-start.82 = (bf16[4,512,512]{2,1,0:T(8,128)(2,1)S(1)}, bf16[4,512,512]{2,1,0:T(8,128)(2,1)S(1)}, u32[]{:S(2)}, u32[]{:S(2)}) collective-permute-start(bf16[4,512,512]{2,1,0:T(8,128)(2,1)S(1)} %add_convert_fusion.8), channel_id=1, source_target_pairs={{2,0},{4,6},{3,1},{5,7},{10,8},{12,14},{11,9},{13,15},{18,16},{20,... | collective-permute-start | bytes 6291464 | tf_op jit(solution)/shard_map/ppermute | solution.py:116
  565.5 97.5 %collective-permute-start.45 = (bf16[512,2048]{1,0:T(8,128)(2,1)S(1)}, bf16[512,2048]{1,0:T(8,128)(2,1)S(1)}, u32[]{:S(2)}, u32[]{:S(2)}) collective-permute-start(bf16[512,2048]{1,0:T(8,128)(2,1)S(1)} %pad_maximum_fusion.8), channel_id=1, source_target_pairs={{0,8},{8,0},{16,24},{24,16},{1,9},{9,1},{17,25},{25,17},{2,10},{10... | collective-permute-start | bytes 6291464 | tf_op jit(solution)/shard_map/ppermute | solution.py:116
  588.3 165.6 %collective-permute-start.97 = (bf16[256,4096]{1,0:T(8,128)(2,1)}, bf16[256,4096]{1,0:T(8,128)(2,1)}, u32[]{:S(2)}, u32[]{:S(2)}) collective-permute-start(bf16[256,4096]{1,0:T(8,128)(2,1)} %add_convert_fusion.5), channel_id=1, source_target_pairs={{2,4},{4,2},{3,5},{5,3},{10,12},{12,10},{11,13},{13,11},{18,20},{2... | collective-permute-start | bytes 6291464 | tf_op jit(solution)/shard_map/ppermute | solution.py:116
  599.8 158.7 %collective-permute-start.75 = (bf16[256,4096]{1,0:T(8,128)(2,1)}, bf16[256,4096]{1,0:T(8,128)(2,1)}, u32[]{:S(2)}, u32[]{:S(2)}) collective-permute-start(bf16[256,4096]{1,0:T(8,128)(2,1)} %constant_dynamic-update-slice_fusion.9), channel_id=1, source_target_pairs={{0,2},{6,4},{1,3},{7,5},{8,10},{14,12},{9,11},{15,13},{16,18},{22,... | collective-permute-start | bytes 6291464 | tf_op jit(solution)/shard_map/ppermute | solution.py:116
  736.5 68.5 %collective-permute-start.93 = (bf16[256,4096]{1,0:T(8,128)(2,1)}, bf16[256,4096]{1,0:T(8,128)(2,1)}, u32[]{:S(2)}, u32[]{:S(2)}) collective-permute-start(bf16[256,4096]{1,0:T(8,128)(2,1)} %constant_dynamic-update-slice_fusion.3), channel_id=1, source_target_pairs={{0,2},{6,4},{1,3},{7,5},{8,10},{14,12},{9,11},{15,13},{16,18},{22,... | collective-permute-start | bytes 6291464 | tf_op jit(solution)/shard_map/ppermute | solution.py:116
  744.0 97.4 %collective-permute-start.48 = (bf16[512,2048]{1,0:T(8,128)(2,1)}, bf16[512,2048]{1,0:T(8,128)(2,1)}, u32[]{:S(2)}, u32[]{:S(2)}) collective-permute-start(bf16[512,2048]{1,0:T(8,128)(2,1)} %convolution_convert_fusion.6), channel_id=1, source_target_pairs={{0,8},{8,0},{16,24},{24,16},{1,9},{9,1},{17,25},{25,17},{2,10},{10... | collective-permute-start | bytes 6291464 | tf_op jit(solution)/shard_map/ppermute | solution.py:116
  758.5 127.0 %collective-permute-start.102 = (bf16[256,4096]{1,0:T(8,128)(2,1)}, bf16[256,4096]{1,0:T(8,128)(2,1)}, u32[]{:S(2)}, u32[]{:S(2)}) collective-permute-start(bf16[256,4096]{1,0:T(8,128)(2,1)} %add_convert_fusion.1), channel_id=1, source_target_pairs={{2,0},{4,6},{3,1},{5,7},{10,8},{12,14},{11,9},{13,15},{18,16},{20,... | collective-permute-start | bytes 6291464 | tf_op jit(solution)/shard_map/ppermute | solution.py:116
  787.0 100.3 %collective-permute-start.79 = (bf16[256,4096]{1,0:T(8,128)(2,1)}, bf16[256,4096]{1,0:T(8,128)(2,1)}, u32[]{:S(2)}, u32[]{:S(2)}) collective-permute-start(bf16[256,4096]{1,0:T(8,128)(2,1)} %add_convert_fusion.11), channel_id=1, source_target_pairs={{2,4},{4,2},{3,5},{5,3},{10,12},{12,10},{11,13},{13,11},{18,20},{2... | collective-permute-start | bytes 6291464 | tf_op jit(solution)/shard_map/ppermute | solution.py:116
  819.5 72.9 %collective-permute-start.94 = (bf16[256,4096]{1,0:T(8,128)(2,1)}, bf16[256,4096]{1,0:T(8,128)(2,1)}, u32[]{:S(2)}, u32[]{:S(2)}) collective-permute-start(bf16[256,4096]{1,0:T(8,128)(2,1)} %constant_dynamic-update-slice_fusion.6), channel_id=1, source_target_pairs={{0,2},{6,4},{1,3},{7,5},{8,10},{14,12},{9,11},{15,13},{16,18},{22,... | collective-permute-start | bytes 6291464 | tf_op jit(solution)/shard_map/ppermute | solution.py:116
  822.9 60.3 %collective-permute-start.77 = (bf16[256,1536]{1,0:T(8,128)(2,1)}, bf16[256,1536]{1,0:T(8,128)(2,1)}, u32[]{:S(2)}, u32[]{:S(2)}) collective-permute-start(bf16[256,1536]{1,0:T(8,128)(2,1)} %dynamic_update_slice.279), channel_id=1, source_target_pairs={{0,2},{6,4},{1,3},{7,5},{8,10},{14,12},{9,11},{15,13},{16,18},{22,... | collective-permute-start | bytes 2359304 | tf_op jit(solution)/shard_map/ppermute | solution.py:116
  841.4 67.2 %collective-permute-start.98 = (bf16[256,4096]{1,0:T(8,128)(2,1)}, bf16[256,4096]{1,0:T(8,128)(2,1)S(1)}, u32[]{:S(2)}, u32[]{:S(2)}) collective-permute-start(bf16[256,4096]{1,0:T(8,128)(2,1)} %add_convert_fusion.6), channel_id=1, source_target_pairs={{2,4},{4,2},{3,5},{5,3},{10,12},{12,10},{11,13},{13,11},{18,20},{2... | collective-permute-start | bytes 6291464 | tf_op jit(solution)/shard_map/ppermute | solution.py:116
  891.1 101.2 %collective-permute-start.83 = (bf16[256,4096]{1,0:T(8,128)(2,1)S(1)}, bf16[256,4096]{1,0:T(8,128)(2,1)S(1)}, u32[]{:S(2)}, u32[]{:S(2)}) collective-permute-start(bf16[256,4096]{1,0:T(8,128)(2,1)S(1)} %add_convert_fusion.9), channel_id=1, source_target_pairs={{2,0},{4,6},{3,1},{5,7},{10,8},{12,14},{11,9},{13,15},{18,16},{20,... | collective-permute-start | bytes 6291464 | tf_op jit(solution)/shard_map/ppermute | solution.py:116
  909.8 77.2 %collective-permute-start.81 = (bf16[256,1536]{1,0:T(8,128)(2,1)S(1)}, bf16[256,1536]{1,0:T(8,128)(2,1)S(1)}, u32[]{:S(2)}, u32[]{:S(2)}) collective-permute-start(bf16[256,1536]{1,0:T(8,128)(2,1)S(1)} %add_convert_fusion.19), channel_id=1, source_target_pairs={{2,4},{4,2},{3,5},{5,3},{10,12},{12,10},{11,13},{13,11},{18,20},{2... | collective-permute-start | bytes 2359304 | tf_op jit(solution)/shard_map/ppermute | solution.py:116
  935.8 62.4 %collective-permute-start.99 = (bf16[256,4096]{1,0:T(8,128)(2,1)S(1)}, bf16[256,4096]{1,0:T(8,128)(2,1)S(1)}, u32[]{:S(2)}, u32[]{:S(2)}) collective-permute-start(bf16[256,4096]{1,0:T(8,128)(2,1)S(1)} %add_convert_fusion.7), channel_id=1, source_target_pairs={{2,4},{4,2},{3,5},{5,3},{10,12},{12,10},{11,13},{13,11},{18,20},{2... | collective-permute-start | bytes 6291464 | tf_op jit(solution)/shard_map/ppermute | solution.py:116
  936.6 63.2 %collective-permute-start.103 = (bf16[256,4096]{1,0:T(8,128)(2,1)S(1)}, bf16[256,4096]{1,0:T(8,128)(2,1)S(1)}, u32[]{:S(2)}, u32[]{:S(2)}) collective-permute-start(bf16[256,4096]{1,0:T(8,128)(2,1)S(1)} %add_convert_fusion.2), channel_id=1, source_target_pairs={{2,0},{4,6},{3,1},{5,7},{10,8},{12,14},{11,9},{13,15},{18,16},{20,... | collective-permute-start | bytes 6291464 | tf_op jit(solution)/shard_map/ppermute | solution.py:116
  999.8 78.5 %collective-permute-start.104 = (bf16[256,4096]{1,0:T(8,128)(2,1)S(1)}, bf16[256,4096]{1,0:T(8,128)(2,1)S(1)}, u32[]{:S(2)}, u32[]{:S(2)}) collective-permute-start(bf16[256,4096]{1,0:T(8,128)(2,1)S(1)} %add_convert_fusion.3), channel_id=1, source_target_pairs={{2,0},{4,6},{3,1},{5,7},{10,8},{12,14},{11,9},{13,15},{18,16},{20,... | collective-permute-start | bytes 6291464 | tf_op jit(solution)/shard_map/ppermute | solution.py:116
  1020.1 58.0 %collective-permute-start.85 = (bf16[256,1536]{1,0:T(8,128)(2,1)S(1)}, bf16[256,1536]{1,0:T(8,128)(2,1)S(1)}, u32[]{:S(2)}, u32[]{:S(2)}) collective-permute-start(bf16[256,1536]{1,0:T(8,128)(2,1)S(1)} %add_convert_fusion.18), channel_id=1, source_target_pairs={{2,0},{4,6},{3,1},{5,7},{10,8},{12,14},{11,9},{13,15},{18,16},{20,... | collective-permute-start | bytes 2359304 | tf_op jit(solution)/shard_map/ppermute | solution.py:116
  (170 other events, 3231.8 us)
where the time goes:
time: 1110 us; the launch traced here: 1100 us
  waiting for transfers between devices  538 us (48%)
  starting transfers between devices  186 us (17%)
  local copies, waits for them, and re-layouts  151 us (14%)
  matrix products  125 us (11%)
  other arithmetic  95.6 us (9%)
    ppermute x104, waiting for transfers between devices, send(): out = lax.ppermute(after(v, *held), axis, perm)  490 us
    ppermute x104, starting transfers between devices, send(): out = lax.ppermute(after(v, *held), axis, perm)  182 us
    ppermute x2, waiting for transfers between devices, body(): lax.ppermute(gain_sum, 'ctx', [(k, k ^ step) for k in range(n_ctx)])  48.4 us
    dynamic_update_slice x40, local copies, waits for them, and re-layouts, finish_rows(): lax.dynamic_update_slice(mine, value[:, low:low + w], (0, base + k * w))  44.3 us
    dot_general x8, matrix products, dot_bt(): lax.dot_general(a, b, (((1,), (1,)), ((), ())), preferred_element_type=F32)  35.5 us
    dot_general x7, matrix products, dot(): return jnp.dot(a, b, preferred_element_type=F32)  32.6 us
    dot_general x6, matrix products, dot_t(): lax.dot_general(a, b, (((0,), (0,)), ((), ())), preferred_element_type=F32)  27.3 us
  transfers between devices with their start and end apart: 106, of which 46 were waited for; matrix products, arithmetic and copies ran while one was open for 26% of the time, Pallas kernels for 0%

commit v1 on v0

--- a/solution.py
+++ b/solution.py
@@ -3,6 +3,7 @@
 import jax
 import jax.numpy as jnp
 from jax import lax
+from jax.experimental import pallas as pl
 from jax.sharding import PartitionSpec as P
 
 
@@ -67,6 +68,125 @@
 
 def dot_bt(a, b):
     return lax.dot_general(a, b, (((1,), (1,)), ((), ())), preferred_element_type=F32)
+
+
+def visible(qseg_ref, kseg_ref, rows, n):
+    qseg = qseg_ref[0]
+    out = [qseg == kseg_ref[0, s : s + 1, :] for s in range(n)]
+    at = lax.broadcasted_iota(jnp.int32, (rows, rows), 0)
+    to = lax.broadcasted_iota(jnp.int32, (rows, rows), 1)
+    out[0] = out[0] & (to <= at)
+    return out
+
+
+def attention_forward(q, kvs, qseg, kseg, hq, hk, score_scale):
+    groups, rows, _ = qseg.shape
+    n, share, kw = len(kvs), hq // hk, hk * HD
+
+    def kernel(q_ref, *refs):
+        kv_refs, (qseg_ref, kseg_ref, o_ref, lse_ref) = refs[:n], refs[n:]
+        seen = visible(qseg_ref, kseg_ref, rows, n)
+        outs, lses = [], []
+        for h in range(hq):
+            g = h // share
+            qh = q_ref[:, h * HD : (h + 1) * HD]
+            scores = [
+                jnp.where(
+                    seen[s], dot_bt(qh, kv_refs[s][:, g * HD : (g + 1) * HD]) * score_scale, -1e30
+                )
+                for s in range(n)
+            ]
+            top = scores[0].max(-1, keepdims=True)
+            for s in range(1, n):
+                top = jnp.maximum(top, scores[s].max(-1, keepdims=True))
+            weights = [jnp.exp(sc - top) for sc in scores]
+            total = sum(w.sum(-1, keepdims=True) for w in weights)
+            scale = 1.0 / total
+            outs.append(
+                sum(
+                    dot((weights[s] * scale).astype(BF), kv_refs[s][:, kw + g * HD : kw + (g + 1) * HD])
+                    for s in range(n)
+                )
+            )
+            lses.append(top + jnp.log(total))
+        o_ref[...] = jnp.concatenate(outs, axis=1).astype(BF)
+        lse_ref[0] = jnp.concatenate(lses, axis=1)
+
+    return pl.pallas_call(
+        kernel,
+        grid=(groups,),
+        in_specs=[pl.BlockSpec((rows, hq * HD), lambda b: (b, 0))]
+        + [pl.BlockSpec((rows, 2 * kw), lambda b: (b, 0))] * n
+        + [
+            pl.BlockSpec((1, rows, 1), lambda b: (b, 0, 0)),
+            pl.BlockSpec((1, n, rows), lambda b: (b, 0, 0)),
+        ],
+        out_specs=[
+            pl.BlockSpec((rows, hq * HD), lambda b: (b, 0)),
+            pl.BlockSpec((1, rows, hq), lambda b: (b, 0, 0)),
+        ],
+        out_shape=[
+            jax.ShapeDtypeStruct((groups * rows, hq * HD), BF),
+            jax.ShapeDtypeStruct((groups, rows, hq), F32),
+        ],
+        name="attention_forward",
+    )(q, *kvs, qseg, kseg)
+
+
+def attention_backward(q, kvs, qseg, kseg, lse, attended, delta, hq, hk, score_scale):
+    groups, rows, _ = qseg.shape
+    n, share, kw = len(kvs), hq // hk, hk * HD
+
+    def kernel(q_ref, *refs):
+        kv_refs = refs[:n]
+        qseg_ref, kseg_ref, lse_ref, o_ref, d_ref, dq_ref = refs[n : n + 6]
+        dkv_refs = refs[n + 6 :]
+        seen = visible(qseg_ref, kseg_ref, rows, n)
+        dqs = []
+        back = [[[0.0] * hk, [0.0] * hk] for _ in range(n)]
+        for h in range(hq):
+            g, own = h // share, slice(h * HD, (h + 1) * HD)
+            qh, dh = q_ref[:, own], d_ref[:, own]
+            inner = jnp.sum(o_ref[:, own].astype(F32) * dh.astype(F32), axis=-1, keepdims=True)
+            log_total = lse_ref[0, :, h : h + 1]
+            dq = 0.0
+            for s in range(n):
+                key = kv_refs[s][:, g * HD : (g + 1) * HD]
+                value = kv_refs[s][:, kw + g * HD : kw + (g + 1) * HD]
+                scores = jnp.where(seen[s], dot_bt(qh, key) * score_scale, -1e30)
+                prob = jnp.exp(scores - log_total)
+                grad = (prob * (dot_bt(dh, value) - inner) * score_scale).astype(BF)
+                dq = dq + dot(grad, key)
+                back[s][0][g] = back[s][0][g] + dot_t(grad, qh)
+                back[s][1][g] = back[s][1][g] + dot_t(prob.astype(BF), dh)
+            dqs.append(dq)
+        dq_ref[...] = jnp.concatenate(dqs, axis=1)
+        for s in range(n):
+            dkv_refs[s][...] = jnp.concatenate(back[s][0] + back[s][1], axis=1).astype(
+                dkv_refs[s].dtype
+            )
+
+    wide = pl.BlockSpec((rows, hq * HD), lambda b: (b, 0))
+    pair = pl.BlockSpec((rows, 2 * kw), lambda b: (b, 0))
+    return pl.pallas_call(
+        kernel,
+        grid=(groups,),
+        in_specs=[wide]
+        + [pair] * n
+        + [
+            pl.BlockSpec((1, rows, 1), lambda b: (b, 0, 0)),
+            pl.BlockSpec((1, n, rows), lambda b: (b, 0, 0)),
+            pl.BlockSpec((1, rows, hq), lambda b: (b, 0, 0)),
+            wide,
+            wide,
+        ],
+        out_specs=[wide] + [pair] * n,
+        out_shape=[jax.ShapeDtypeStruct((groups * rows, hq * HD), F32)]
+        + [
+            jax.ShapeDtypeStruct((groups * rows, 2 * kw), F32 if s == 0 else BF) for s in range(n)
+        ],
+        name="attention_backward",
+    )(q, *kvs, qseg, kseg, lse, attended, delta)
 
 
 def after(value, *deps):
@@ -94,7 +214,6 @@
     tp = math.gcd(n_fsdp, kv_local)
     n_out = n_fsdp // tp
     hq, hk = heads_local // tp, kv_local // tp
-    share = hq // hk
     ff_part = w_gate.shape[1] // tp
     d_blk = w_query.shape[0]
     score_scale = 1.0 / math.sqrt(HD)
@@ -249,31 +368,16 @@
     reach = min(-(-(MAXLEN - 1) // rows), n_ctx - 1)
     kv_own = jnp.concatenate([key_rot.reshape(tp * rows, k_cols), value_rows], axis=1)
     kv_blocks = [kv_own] + [shift(kv_own, s) for s in range(1, reach + 1)]
-    kv_all = jnp.concatenate(
-        [v.reshape(tp, 1, rows, 2, hk, HD) for v in kv_blocks], axis=1
-    ).reshape(tp, (reach + 1) * rows, 2, hk, HD)
     key_index = jnp.concatenate(
         [(z - s) * rows + jnp.arange(rows, dtype=jnp.int32) for s in range(reach + 1)]
     )
     k_seg, _ = layout(lengths, key_index)
-    allowed = (
-        (q_seg[:, :, None] == k_seg[:, None, :])
-        & (key_index[None, None, :] <= local_index[None, :, None])
-        & (key_index[None, None, :] >= 0)
-    )[:, None, None]
-    q_h = query_rot.reshape(tp, rows, hk, share, HD).transpose(0, 2, 3, 1, 4)
-    k_h = kv_all[:, :, 0].transpose(0, 2, 1, 3)
-    v_h = kv_all[:, :, 1].transpose(0, 2, 1, 3)
-
-    scores = jnp.einsum("bgrtd,bgsd->bgrts", q_h, k_h, preferred_element_type=F32) * score_scale
-    masked = jnp.where(allowed, scores, -1e30)
-    row_max = jnp.max(masked, axis=-1, keepdims=True)
-    exp_total = jnp.sum(jnp.where(allowed, jnp.exp(masked - row_max), 0.0), axis=-1, keepdims=True)
-    log_total = row_max + jnp.log(exp_total)
-    prob = jnp.where(allowed, jnp.exp(masked - log_total), 0.0)
-    prob_low = prob.astype(BF)
-    attended = jnp.einsum("bgrts,bgsd->bgrtd", prob_low, v_h, preferred_element_type=F32).astype(BF)
-    attended_rows = attended.transpose(0, 3, 1, 2, 4).reshape(tp * rows, hq * HD)
+    k_seg = jnp.where(key_index[None, :] >= 0, k_seg, -1).reshape(tp, reach + 1, rows)
+    q_seg = q_seg[:, :, None]
+    query_rows = query_rot.reshape(tp * rows, q_cols)
+    attended_rows, log_total = attention_forward(
+        query_rows, kv_blocks, q_seg, k_seg, hq, hk, score_scale
+    )
     residual = input_wide + reduce_rows([(attended_rows, out_full)], dot)
 
     cot_all = gather_rows(cotangent)
@@ -284,7 +388,10 @@
     sigmoid_gate = jax.nn.sigmoid(gate_pre)
     silu_gate = gate_pre * sigmoid_gate
     activation = (silu_gate * up_pre).astype(BF)
-    act_delta = dot_bt(cot_all, down_full)
+    down_parts = [
+        dot_t(activation[:, at : at + half], cot_all).astype(BF) for at in range(0, ff_part, half)
+    ]
+    act_delta = dot_bt(cot_all, after(down_full, *down_parts))
     silu_slope = sigmoid_gate * (1.0 + gate_pre * (1.0 - sigmoid_gate))
     gate_delta = (act_delta * up_pre * silu_slope).astype(BF)
     up_delta = (act_delta * silu_gate).astype(BF)
@@ -340,10 +447,6 @@
             mine = lax.dynamic_update_slice(mine, value[None], (k, 0, 0))
         return mine
 
-    def grad_cols(left, right, n, chunks):
-        b = left.shape[1] // chunks
-        return finish_cols(dot_t(left[:, n * b : (n + 1) * b], right).astype(BF))
-
     def grad_rows(part, widths, n, chunks):
         b = d_blk // chunks
         return finish_rows(part.reshape(n_fsdp, chunks, b, part.shape[1])[:, n], widths)
@@ -357,39 +460,25 @@
 
     up_part = dot_t(normed_two, up_delta).astype(BF)
     gate_part = dot_t(normed_two, gate_delta).astype(BF)
-    down_low_grad = ctx_total(grad_cols(activation, cot_all, 0, 2))
-    down_high_grad = ctx_total(grad_cols(activation, cot_all, 1, 2))
+    down_grads = [ctx_total(finish_cols(part)) for part in down_parts]
     normed_two_delta = reduce_rows([(gate_delta, gate_full), (up_delta, up_full)], dot_bt, "x")
     gain_two_term, residual_back = norm_backward(normed_two_delta, unit_two, rstd_two, gain_two)
     residual_delta = cotangent.astype(F32) + residual_back
-    up_low_grad = ctx_total(grad_rows(up_part, (ff_part,), 0, 2))
+    up_grads = [ctx_total(grad_rows(up_part, (ff_part,), n, 2)) for n in range(2)]
     residual_low = gather_rows(residual_delta.astype(BF), "x")
-    up_high_grad = ctx_total(grad_rows(up_part, (ff_part,), 1, 2))
-    gate_low_grad = ctx_total(grad_rows(gate_part, (ff_part,), 0, 2))
-    output_grad = ctx_total(grad_cols(attended_rows, residual_low, 0, 1))
-    gate_high_grad = ctx_total(grad_rows(gate_part, (ff_part,), 1, 2))
+    gate_grads = [ctx_total(grad_rows(gate_part, (ff_part,), n, 2)) for n in range(2)]
+    output_grad = ctx_total(finish_cols(dot_t(attended_rows, residual_low).astype(BF)))
 
     attended_delta = dot_bt(residual_low, out_full).astype(BF)
-    delta_h = attended_delta.reshape(tp, rows, hk, share, HD).transpose(0, 2, 3, 1, 4)
-    inner_rows = jnp.sum(attended.astype(F32) * delta_h.astype(F32), axis=-1, keepdims=True)
-    prob_delta = jnp.einsum("bgrtd,bgsd->bgrts", delta_h, v_h, preferred_element_type=F32)
-    score_delta = (prob * (prob_delta - inner_rows) * score_scale).astype(BF)
-    query_back = jnp.einsum("bgrts,bgsd->bgrtd", score_delta, k_h, preferred_element_type=F32)
-    key_back = jnp.einsum("bgrts,bgrtd->bgsd", score_delta, q_h, preferred_element_type=F32)
-    value_back = jnp.einsum("bgrts,bgrtd->bgsd", prob_low, delta_h, preferred_element_type=F32)
-
-    def to_blocks(v):
-        v = v.transpose(0, 2, 1, 3).reshape(tp, reach + 1, rows, k_cols)
-        return [v[:, s].reshape(tp * rows, k_cols) for s in range(reach + 1)]
-
-    kv_back = [
-        jnp.concatenate([kb, vb], axis=1) for kb, vb in zip(to_blocks(key_back), to_blocks(value_back))
-    ]
+    query_back, *kv_back = attention_backward(
+        query_rows, kv_blocks, q_seg, k_seg, log_total, attended_rows, attended_delta,
+        hq, hk, score_scale,
+    )
     kv_sum = kv_back[0]
     for s in range(1, reach + 1):
-        kv_sum = kv_sum + shift(kv_back[s].astype(BF), -s).astype(F32)
+        kv_sum = kv_sum + shift(kv_back[s], -s).astype(F32)
     query_delta = rotate(
-        query_back.transpose(0, 3, 1, 2, 4).reshape(tp * rows, hq, HD), cosine_table, sine_table, -1.0
+        query_back.reshape(tp * rows, hq, HD), cosine_table, sine_table, -1.0
     ).reshape(tp * rows, q_cols)
     key_delta = rotate(
         kv_sum[:, :k_cols].reshape(tp * rows, hk, HD), cosine_table, sine_table, -1.0
@@ -410,7 +499,7 @@
             terms.reshape(2, n_out, tp * d_blk), "fsdp", scatter_dimension=1, axis_index_groups=outer_groups
         )
     got = exchange(lambda k: cols(terms, k, d_blk), None)
-    gain_sum = sum(value for _, value in got)
+    gain_sum = after(sum(value for _, value in got), *lanes["mid"][-1])
     step = 1
     while step < n_ctx:
         gain_sum = gain_sum + lax.ppermute(gain_sum, "ctx", [(k, k ^ step) for k in range(n_ctx)])
@@ -427,9 +516,9 @@
         qkv_out[:, q_all + k_all :],
         join_cols([output_grad]),
         gain_grads[1],
-        join_rows([gate_low_grad, gate_high_grad]),
-        join_rows([up_low_grad, up_high_grad]),
-        join_cols([down_low_grad, down_high_grad]),
+        join_rows(gate_grads),
+        join_rows(up_grads),
+        join_cols(down_grads),
     )
 
 

time: 1110 us -> 1080 us (0.973)
  local copies, waits for them, and re-layouts: 151 us -> 118 us
  Pallas kernels: 0 us -> 31.3 us
  starting transfers between devices: 186 us -> 214 us
  waiting for transfers between devices: 538 us -> 510 us
  matrix products: 125 us -> 101 us
    ppermute x2, starting transfers between devices: 4.54 us -> 41.9 us  [body(): lax.ppermute(gain_sum, 'ctx', [(k, k ^ step) for k in range(n_ctx)])]
    pallas_call x0 -> x2, Pallas kernels: none -> 31.3 us  [the longest x1 18.8 us: attention_backward(): pl.pallas_call(kernel, grid=(groups,), in_specs=[wide] + [pair] * n + [pl...]
    dot_general x6 -> x0, matrix products: 29.4 us -> none  [the longest x1 8.48 us: body(): jnp.einsum('bgrtd,bgsd->bgrts', delta_h, v_h, preferred_element_type=F32)]
    ppermute x104, waiting for transfers between devices: 490 us -> 470 us  [send(): out = lax.ppermute(after(v, *held), axis, perm)]
    reshape x11 -> x1, local copies, waits for them, and re-layouts: 14.7 us -> 0.79 us  [body(): key_delta = rotate(kv_sum[:, :k_cols].reshape(tp * rows, hk, HD), cosine_...]
  transfers between devices with their start and end apart: 106 -> 106, of which waited for: 46 -> 43; matrix products, arithmetic and copies ran while one was open for 26% -> 21% of each run, Pallas kernels for 0% -> 2%
where the time goes in v1:
time: 1080 us; the launch traced here: 1070 us
  waiting for transfers between devices  510 us (47%)
  starting transfers between devices  214 us (20%)
  local copies, waits for them, and re-layouts  118 us (11%)
  matrix products  101 us (9%)
  other arithmetic  93.5 us (9%)
  Pallas kernels  31.3 us (3%)
    ppermute x104, waiting for transfers between devices, send(): out = lax.ppermute(after(v, *held), axis, perm)  470 us
    ppermute x104, starting transfers between devices, send(): out = lax.ppermute(after(v, *held), axis, perm)  172 us
    dynamic_update_slice x40, local copies, waits for them, and re-layouts, finish_rows(): lax.dynamic_update_slice(mine, value[:, low:low + w], (0, base + k * w))  43 us
    ppermute x2, starting transfers between devices, body(): lax.ppermute(gain_sum, 'ctx', [(k, k ^ step) for k in range(n_ctx)])  41.9 us
    ppermute x2, waiting for transfers between devices, body(): lax.ppermute(gain_sum, 'ctx', [(k, k ^ step) for k in range(n_ctx)])  39.7 us
    dot_general x6, matrix products, dot_t(): lax.dot_general(a, b, (((0,), (0,)), ((), ())), preferred_element_type=F32)  35.9 us
    dot_general x8, matrix products, dot_bt(): lax.dot_general(a, b, (((1,), (1,)), ((), ())), preferred_element_type=F32)  33.1 us
    dot_general x7, matrix products, dot(): return jnp.dot(a, b, preferred_element_type=F32)  32 us
  transfers between devices with their start and end apart: 106, of which 43 were waited for; matrix products, arithmetic and copies ran while one was open for 21% of the time, Pallas kernels for 2%

profile of v1, /device:TPU:0, one launch (start us, length us, event | category | flops | bytes accessed | tf_op | source)
XLA Modules:
  0.0 1071.4 jit_solution(2108276825304467039)
XLA Ops:
  17.8 18.2 %collective-permute-done.3 = bf16[256,2048]{1,0:T(8,128)(2,1)} collective-permute-done((bf16[256,2048]{1,0:T(8,128)(2,1)S(1)}, bf16[256,2048]{1,0:T(8,128)(2,1)}, u32[]{:S(2)}, u32[]{:S(2)}) %collective-permute-start.3) | collective-permute-done | bytes 1048608 | tf_op jit(solution)/shard_map/ppermute | solution.py:235
  91.1 12.5 %attention_forward.1 = (bf16[1024,256]{1,0:T(8,128)(2,1)}, f32[4,256,4]{2,1,0:T(8,128)}) custom-call(bf16[1024,256]{1,0:T(8,128)(2,1)} %copy.60.q_ref, bf16[1024,128]{1,0:T(8,128)(2,1)} %copy-done.26, bf16[1024,128]{1,0:T(8,128)(2,1)} %copy-done.34, bf16[1024,128]{1,0:T(8,128)(2,1)} %collective-permute-done.11.refs_2_, s32[4,256,1]{2,1,0:T(8,128)} %copy.61.refs_3_, ...), custom_call_target="tpu_custom_call" | custom-call | tf_op jit(solution)/shard_map/attention_forward/pallas_call | solution.py:115
  111.2 24.6 %collective-permute-done.16 = bf16[256,2048]{1,0:T(8,128)(2,1)S(1)} collective-permute-done((bf16[256,2048]{1,0:T(8,128)(2,1)S(1)}, bf16[256,2048]{1,0:T(8,128)(2,1)S(1)}, u32[]{:S(2)}, u32[]{:S(2)}) %collective-permute-start.16) | collective-permute-done | bytes 1048608 | tf_op jit(solution)/shard_map/ppermute | solution.py:235
  144.8 17.0 %collective-permute-done.17 = bf16[256,2048]{1,0:T(8,128)(2,1)} collective-permute-done((bf16[256,2048]{1,0:T(8,128)(2,1)}, bf16[256,2048]{1,0:T(8,128)(2,1)}, u32[]{:S(2)}, u32[]{:S(2)}) %collective-permute-start.17) | collective-permute-done | bytes 1048608 | tf_op jit(solution)/shard_map/ppermute | solution.py:235
  193.5 16.3 %collective-permute-done.18 = bf16[256,2048]{1,0:T(8,128)(2,1)} collective-permute-done((bf16[256,2048]{1,0:T(8,128)(2,1)}, bf16[256,2048]{1,0:T(8,128)(2,1)}, u32[]{:S(2)}, u32[]{:S(2)}) %collective-permute-start.18) | collective-permute-done | bytes 1048608 | tf_op jit(solution)/shard_map/ppermute | solution.py:235
  211.5 20.7 %collective-permute-done.23 = bf16[512,1024]{1,0:T(8,128)(2,1)} collective-permute-done((bf16[512,1024]{1,0:T(8,128)(2,1)S(1)}, bf16[512,1024]{1,0:T(8,128)(2,1)}, u32[]{:S(2)}, u32[]{:S(2)}) %collective-permute-start.23) | collective-permute-done | bytes 1048608 | tf_op jit(solution)/shard_map/ppermute | solution.py:235
  240.4 12.3 %collective-permute-done.20 = bf16[512,1024]{1,0:T(8,128)(2,1)} collective-permute-done((bf16[512,1024]{1,0:T(8,128)(2,1)S(1)}, bf16[512,1024]{1,0:T(8,128)(2,1)}, u32[]{:S(2)}, u32[]{:S(2)}) %collective-permute-start.20) | collective-permute-done | bytes 1048608 | tf_op jit(solution)/shard_map/ppermute | solution.py:235
  260.9 9.0 collective-permute-done.28
  275.4 17.1 %collective-permute-done.25 = bf16[512,1024]{1,0:T(8,128)(2,1)} collective-permute-done((bf16[512,1024]{1,0:T(8,128)(2,1)}, bf16[512,1024]{1,0:T(8,128)(2,1)}, u32[]{:S(2)}, u32[]{:S(2)}) %collective-permute-start.25) | collective-permute-done | bytes 1048608 | tf_op jit(solution)/shard_map/ppermute | solution.py:235
  293.8 21.1 %collective-permute-done.22 = bf16[512,1024]{1,0:T(8,128)(2,1)} collective-permute-done((bf16[512,1024]{1,0:T(8,128)(2,1)}, bf16[512,1024]{1,0:T(8,128)(2,1)}, u32[]{:S(2)}, u32[]{:S(2)}) %collective-permute-start.22) | collective-permute-done | bytes 1048608 | tf_op jit(solution)/shard_map/ppermute | solution.py:235
  324.8 10.6 multiply_convert_fusion.2
  348.1 11.1 %multiply_convert_fusion.1 = (bf16[1024,1024]{1,0:T(8,128)(2,1)}, bf16[1024,1024]{1,0:T(8,128)(2,1)S(1)}) fusion(f32[1024,1024]{1,0:T(8,128)} %copy-done.64, f32[1024,1024]{1,0:T(8,128)} %get-tuple-element.218, bf16[1024,2048]{1,0:T(8,128)(2,1)} %constant_dynamic-update-slice_fusion.34, bf16[1024,2048]{1,0:T(8,128)(2,1)S(1)} %pad_maximum_fusion.2), kind=kOutput, calls=%fused_computation.24 | convolution fusion | flops 4308598784 | bytes 20971520 | tf_op jit(solution)/shard_map/dot_general | solution.py:70
  410.6 12.4 %collective-permute-done.38 = bf16[512,512]{1,0:T(8,128)(2,1)S(1)} collective-permute-done((bf16[512,512]{1,0:T(8,128)(2,1)S(1)}, bf16[512,512]{1,0:T(8,128)(2,1)S(1)}, u32[]{:S(2)}, u32[]{:S(2)}) %collective-permute-start.38) | collective-permute-done | bytes 524320 | tf_op jit(solution)/shard_map/ppermute | solution.py:235
  452.2 16.0 %collective-permute-done.40 = bf16[256,2048]{1,0:T(8,128)(2,1)S(1)} collective-permute-done((bf16[256,2048]{1,0:T(8,128)(2,1)S(1)}, bf16[256,2048]{1,0:T(8,128)(2,1)S(1)}, u32[]{:S(2)}, u32[]{:S(2)}) %collective-permute-start.40) | collective-permute-done | bytes 1048608 | tf_op jit(solution)/shard_map/ppermute | solution.py:235
  475.2 40.7 %collective-permute-done.89 = bf16[4,512,512]{2,1,0:T(8,128)(2,1)} collective-permute-done((bf16[4,512,512]{2,1,0:T(8,128)(2,1)S(1)}, bf16[4,512,512]{2,1,0:T(8,128)(2,1)}, u32[]{:S(2)}, u32[]{:S(2)}) %collective-permute-start.89) | collective-permute-done | bytes 2097184 | tf_op jit(solution)/shard_map/ppermute | solution.py:235
  522.5 12.2 %collective-permute-done.44 = bf16[256,1024]{1,0:T(8,128)(2,1)S(1)} collective-permute-done((bf16[256,1024]{1,0:T(8,128)(2,1)S(1)}, bf16[256,1024]{1,0:T(8,128)(2,1)S(1)}, u32[]{:S(2)}, u32[]{:S(2)}) %collective-permute-start.44) | collective-permute-done | bytes 524320 | tf_op jit(solution)/shard_map/ppermute | solution.py:235
  569.6 19.9 %collective-permute-done.74 = bf16[256,4096]{1,0:T(8,128)(2,1)S(1)} collective-permute-done((bf16[256,4096]{1,0:T(8,128)(2,1)S(1)}, bf16[256,4096]{1,0:T(8,128)(2,1)S(1)}, u32[]{:S(2)}, u32[]{:S(2)}) %collective-permute-start.74) | collective-permute-done | bytes 2097184 | tf_op jit(solution)/shard_map/ppermute | solution.py:235
  593.4 10.2 collective-permute-done.52
  606.0 21.2 %collective-permute-done.90 = bf16[256,4096]{1,0:T(8,128)(2,1)S(1)} collective-permute-done((bf16[256,4096]{1,0:T(8,128)(2,1)S(1)}, bf16[256,4096]{1,0:T(8,128)(2,1)S(1)}, u32[]{:S(2)}, u32[]{:S(2)}) %collective-permute-start.90) | collective-permute-done | bytes 2097184 | tf_op jit(solution)/shard_map/ppermute | solution.py:235
  632.1 9.1 collective-permute-done.54
  641.2 23.0 %collective-permute-start.75 = (bf16[256,4096]{1,0:T(8,128)(2,1)}, bf16[256,4096]{1,0:T(8,128)(2,1)}, u32[]{:S(2)}, u32[]{:S(2)}) collective-permute-start(bf16[256,4096]{1,0:T(8,128)(2,1)} %constant_dynamic-update-slice_fusion.9), channel_id=1, source_target_pairs={{0,2},{6,4},{1,3},{7,5},{8,10},{14,12},{9,11},{15,13},{16,18},{22,... | collective-permute-start | bytes 6291464 | tf_op jit(solution)/shard_map/ppermute | solution.py:235
  673.0 18.8 %attention_backward.1 = (f32[1024,256]{1,0:T(8,128)}, f32[1024,128]{1,0:T(8,128)}, bf16[1024,128]{1,0:T(8,128)(2,1)}, bf16[1024,128]{1,0:T(8,128)(2,1)}) custom-call(bf16[1024,256]{1,0:T(8,128)(2,1)} %copy.60.q_ref, bf16[1024,128]{1,0:T(8,128)(2,1)} %copy-done.26, bf16[1024,128]{1,0:T(8,128)(2,1)} %copy-done.34, ...), custom_call_target="tpu_custom_call" | custom-call | tf_op jit(solution)/shard_map/attention_backward/pallas_call | solution.py:171
  745.4 17.7 %collective-permute-start.91 = (bf16[256,4096]{1,0:T(8,128)(2,1)}, bf16[256,4096]{1,0:T(8,128)(2,1)}, u32[]{:S(2)}, u32[]{:S(2)}) collective-permute-start(bf16[256,4096]{1,0:T(8,128)(2,1)} %constant_dynamic-update-slice_fusion.3), channel_id=1, source_target_pairs={{0,2},{6,4},{1,3},{7,5},{8,10},{14,12},{9,11},{15,13},{16,18},{22,... | collective-permute-start | bytes 6291464 | tf_op jit(solution)/shard_map/ppermute | solution.py:235
  833.4 11.9 %collective-permute-done.92 = bf16[256,1536]{1,0:T(8,128)(2,1)S(1)} collective-permute-done((bf16[256,1536]{1,0:T(8,128)(2,1)}, bf16[256,1536]{1,0:T(8,128)(2,1)S(1)}, u32[]{:S(2)}, u32[]{:S(2)}) %collective-permute-start.92) | collective-permute-done | bytes 786464 | tf_op jit(solution)/shard_map/ppermute | solution.py:235
  854.9 10.3 collective-permute-done.77
  873.7 17.0 %collective-permute-done.98 = bf16[256,4096]{1,0:T(8,128)(2,1)S(1)} collective-permute-done((bf16[256,4096]{1,0:T(8,128)(2,1)S(1)}, bf16[256,4096]{1,0:T(8,128)(2,1)S(1)}, u32[]{:S(2)}, u32[]{:S(2)}) %collective-permute-start.98) | collective-permute-done | bytes 2097184 | tf_op jit(solution)/shard_map/ppermute | solution.py:235
  900.5 20.0 %collective-permute-done.64 = bf16[256,2048]{1,0:T(8,128)(2,1)S(1)} collective-permute-done((bf16[256,2048]{1,0:T(8,128)(2,1)S(1)}, bf16[256,2048]{1,0:T(8,128)(2,1)S(1)}, u32[]{:S(2)}, u32[]{:S(2)}) %collective-permute-start.64) | collective-permute-done | bytes 1048608 | tf_op jit(solution)/shard_map/ppermute | solution.py:235
  926.5 41.9 %collective-permute-start.83 = (f32[2,512]{1,0:T(2,128)S(1)}, f32[2,512]{1,0:T(2,128)S(1)}, u32[]{:S(2)}, u32[]{:S(2)}) collective-permute-start(f32[2,512]{1,0:T(2,128)S(1)} %add_add_fusion), channel_id=1, source_target_pairs={{0,2},{2,0},{4,6},{6,4},{1,3},{3,1},{5,7},{7,5},{8,10},{10,8},{12,... | collective-permute-start | bytes 12296 | tf_op jit(solution)/shard_map/ppermute | solution.py:505
  968.6 35.3 %collective-permute-done.83 = f32[2,512]{1,0:T(2,128)S(1)} collective-permute-done((f32[2,512]{1,0:T(2,128)S(1)}, f32[2,512]{1,0:T(2,128)S(1)}, u32[]{:S(2)}, u32[]{:S(2)}) %collective-permute-start.83) | collective-permute-done | bytes 4128 | tf_op jit(solution)/shard_map/ppermute | solution.py:505
  1020.0 16.9 %collective-permute-done.104 = bf16[4,256,512]{2,1,0:T(8,128)(2,1)S(1)} collective-permute-done((bf16[4,256,512]{2,1,0:T(8,128)(2,1)S(1)}, bf16[4,256,512]{2,1,0:T(8,128)(2,1)S(1)}, u32[]{:S(2)}, u32[]{:S(2)}) %collective-permute-start.104) | collective-permute-done | bytes 1048608 | tf_op jit(solution)/shard_map/ppermute | solution.py:235
  1040.0 13.8 %collective-permute-done.100 = bf16[256,1536]{1,0:T(8,128)(2,1)S(1)} collective-permute-done((bf16[256,1536]{1,0:T(8,128)(2,1)S(1)}, bf16[256,1536]{1,0:T(8,128)(2,1)S(1)}, u32[]{:S(2)}, u32[]{:S(2)}) %collective-permute-start.100) | collective-permute-done | bytes 786464 | tf_op jit(solution)/shard_map/ppermute | solution.py:235
  1053.8 14.1 %collective-permute-done.105 = bf16[256,1536]{1,0:T(8,128)(2,1)S(1)} collective-permute-done((bf16[256,1536]{1,0:T(8,128)(2,1)S(1)}, bf16[256,1536]{1,0:T(8,128)(2,1)S(1)}, u32[]{:S(2)}, u32[]{:S(2)}) %collective-permute-start.105) | collective-permute-done | bytes 786464 | tf_op jit(solution)/shard_map/ppermute | solution.py:235
  (567 shorter events, 495.3 us)
Async XLA Ops:
  138.6 50.6 %collective-permute-start.33 = (bf16[256,2048]{1,0:T(8,128)(2,1)S(1)}, bf16[256,2048]{1,0:T(8,128)(2,1)}, u32[]{:S(2)}, u32[]{:S(2)}) collective-permute-start(bf16[256,2048]{1,0:T(8,128)(2,1)S(1)} %copy-done.2), channel_id=1, source_target_pairs={{0,16},{8,24},{16,0},{24,8},{1,17},{9,25},{17,1},{25,9},{2,18},{10... | collective-permute-start | bytes 3145736 | tf_op jit(solution)/shard_map/ppermute | solution.py:235
  176.0 56.2 %collective-permute-start.23 = (bf16[512,1024]{1,0:T(8,128)(2,1)S(1)}, bf16[512,1024]{1,0:T(8,128)(2,1)}, u32[]{:S(2)}, u32[]{:S(2)}) collective-permute-start(bf16[512,1024]{1,0:T(8,128)(2,1)S(1)} %get-tuple-element.135), channel_id=1, source_target_pairs={{0,16},{2,26},{4,20},{6,30},{8,24},{10,18},{12,28},{14,22},{16,0},... | collective-permute-start | bytes 3145736 | tf_op jit(solution)/shard_map/ppermute | solution.py:235
  176.6 60.8 %collective-permute-start.24 = (bf16[512,1024]{1,0:T(8,128)(2,1)S(1)}, bf16[512,1024]{1,0:T(8,128)(2,1)S(1)}, u32[]{:S(2)}, u32[]{:S(2)}) collective-permute-start(bf16[512,1024]{1,0:T(8,128)(2,1)S(1)} %get-tuple-element.133), channel_id=1, source_target_pairs={{0,8},{8,0},{16,24},{24,16},{1,9},{9,1},{17,25},{25,17},{2,10},{10... | collective-permute-start | bytes 3145736 | tf_op jit(solution)/shard_map/ppermute | solution.py:235
  187.2 65.4 %collective-permute-start.20 = (bf16[512,1024]{1,0:T(8,128)(2,1)S(1)}, bf16[512,1024]{1,0:T(8,128)(2,1)}, u32[]{:S(2)}, u32[]{:S(2)}) collective-permute-start(bf16[512,1024]{1,0:T(8,128)(2,1)S(1)} %get-tuple-element.132), channel_id=1, source_target_pairs={{0,16},{2,26},{4,20},{6,30},{8,24},{10,18},{12,28},{14,22},{16,0},... | collective-permute-start | bytes 3145736 | tf_op jit(solution)/shard_map/ppermute | solution.py:235
  192.9 79.4 %collective-permute-start.21 = (bf16[512,1024]{1,0:T(8,128)(2,1)S(1)}, bf16[512,1024]{1,0:T(8,128)(2,1)S(1)}, u32[]{:S(2)}, u32[]{:S(2)}) collective-permute-start(bf16[512,1024]{1,0:T(8,128)(2,1)S(1)} %get-tuple-element.130), channel_id=1, source_target_pairs={{0,8},{8,0},{16,24},{24,16},{1,9},{9,1},{17,25},{25,17},{2,10},{10... | collective-permute-start | bytes 3145736 | tf_op jit(solution)/shard_map/ppermute | solution.py:235
  209.7 106.5 %collective-permute-start.34 = (bf16[512,2048]{1,0:T(8,128)(2,1)S(1)}, bf16[512,2048]{1,0:T(8,128)(2,1)S(1)}, u32[]{:S(2)}, u32[]{:S(2)}) collective-permute-start(bf16[512,2048]{1,0:T(8,128)(2,1)S(1)} %pad_maximum_fusion.7), channel_id=1, source_target_pairs={{0,8},{8,0},{16,24},{24,16},{1,9},{9,1},{17,25},{25,17},{2,10},{10... | collective-permute-start | bytes 6291464 | tf_op jit(solution)/shard_map/ppermute | solution.py:235
  237.4 80.4 %collective-permute-start.19 = (bf16[512,2048]{1,0:T(8,128)(2,1)S(1)}, bf16[512,2048]{1,0:T(8,128)(2,1)}, u32[]{:S(2)}, u32[]{:S(2)}) collective-permute-start(bf16[512,2048]{1,0:T(8,128)(2,1)S(1)} %pad_maximum_fusion.6), channel_id=1, source_target_pairs={{0,8},{8,0},{16,24},{24,16},{1,9},{9,1},{17,25},{25,17},{2,10},{10... | collective-permute-start | bytes 6291464 | tf_op jit(solution)/shard_map/ppermute | solution.py:235
  378.1 60.3 %collective-permute-start.35 = (bf16[512,2048]{1,0:T(8,128)(2,1)}, bf16[512,2048]{1,0:T(8,128)(2,1)}, u32[]{:S(2)}, u32[]{:S(2)}) collective-permute-start(bf16[512,2048]{1,0:T(8,128)(2,1)} %add_convert_fusion.12), channel_id=1, source_target_pairs={{0,8},{8,0},{16,24},{24,16},{1,9},{9,1},{17,25},{25,17},{2,10},{10... | collective-permute-start | bytes 6291464 | tf_op jit(solution)/shard_map/ppermute | solution.py:235
  399.4 47.7 %collective-permute-start.70 = (bf16[256,1024]{1,0:T(8,128)(2,1)}, bf16[256,1024]{1,0:T(8,128)(2,1)}, u32[]{:S(2)}, u32[]{:S(2)}) collective-permute-start(bf16[256,1024]{1,0:T(8,128)(2,1)} %get-tuple-element.151), channel_id=1, source_target_pairs={{0,8},{8,0},{16,24},{24,16},{1,9},{9,1},{17,25},{25,17},{2,10},{10... | collective-permute-start | bytes 1572872 | tf_op jit(solution)/shard_map/ppermute | solution.py:235
  423.0 49.9 %collective-permute-start.73 = (bf16[4,512,512]{2,1,0:T(8,128)(2,1)S(1)}, bf16[4,512,512]{2,1,0:T(8,128)(2,1)}, u32[]{:S(2)}, u32[]{:S(2)}) collective-permute-start(bf16[4,512,512]{2,1,0:T(8,128)(2,1)S(1)} %bitcast_dynamic-update-slice_fusion.6), channel_id=1, source_target_pairs={{0,2},{6,4},{1,3},{7,5},{8,10},{14,12},{9,11},{15,13},{16,18},{22,... | collective-permute-start | bytes 6291464 | tf_op jit(solution)/shard_map/ppermute | solution.py:235
  433.1 82.7 %collective-permute-start.89 = (bf16[4,512,512]{2,1,0:T(8,128)(2,1)S(1)}, bf16[4,512,512]{2,1,0:T(8,128)(2,1)}, u32[]{:S(2)}, u32[]{:S(2)}) collective-permute-start(bf16[4,512,512]{2,1,0:T(8,128)(2,1)S(1)} %bitcast_dynamic-update-slice_fusion), channel_id=1, source_target_pairs={{0,2},{6,4},{1,3},{7,5},{8,10},{14,12},{9,11},{15,13},{16,18},{22,... | collective-permute-start | bytes 6291464 | tf_op jit(solution)/shard_map/ppermute | solution.py:235
  449.7 96.5 %collective-permute-start.32 = (bf16[512,2048]{1,0:T(8,128)(2,1)}, bf16[512,2048]{1,0:T(8,128)(2,1)}, u32[]{:S(2)}, u32[]{:S(2)}) collective-permute-start(bf16[512,2048]{1,0:T(8,128)(2,1)} %convolution_convert_fusion.4), channel_id=1, source_target_pairs={{0,8},{8,0},{16,24},{24,16},{1,9},{9,1},{17,25},{25,17},{2,10},{10... | collective-permute-start | bytes 6291464 | tf_op jit(solution)/shard_map/ppermute | solution.py:235
  468.6 53.1 %collective-permute-start.41 = (bf16[256,2048]{1,0:T(8,128)(2,1)S(1)}, bf16[256,2048]{1,0:T(8,128)(2,1)S(1)}, u32[]{:S(2)}, u32[]{:S(2)}) collective-permute-start(bf16[256,2048]{1,0:T(8,128)(2,1)S(1)} %fusion.13), channel_id=1, source_target_pairs={{0,1},{1,0},{2,3},{3,2},{4,5},{5,4},{6,7},{7,6},{8,9},{9,8},{10,11... | collective-permute-start | bytes 3145736 | tf_op jit(solution)/shard_map/ppermute | solution.py:235
  469.2 49.9 %collective-permute-start.42 = (bf16[256,1024]{1,0:T(8,128)(2,1)S(1)}, bf16[256,1024]{1,0:T(8,128)(2,1)S(1)}, u32[]{:S(2)}, u32[]{:S(2)}) collective-permute-start(bf16[256,1024]{1,0:T(8,128)(2,1)S(1)} %copy-done.41), channel_id=1, source_target_pairs={{0,16},{8,24},{16,0},{24,8},{1,17},{9,25},{17,1},{25,9},{2,18},{10... | collective-permute-start | bytes 1572872 | tf_op jit(solution)/shard_map/ppermute | solution.py:235
  473.0 46.9 %collective-permute-start.43 = (bf16[256,1024]{1,0:T(8,128)(2,1)S(1)}, bf16[256,1024]{1,0:T(8,128)(2,1)S(1)}, u32[]{:S(2)}, u32[]{:S(2)}) collective-permute-start(bf16[256,1024]{1,0:T(8,128)(2,1)S(1)} %get-tuple-element.67), channel_id=1, source_target_pairs={{0,24},{8,16},{16,8},{24,0},{1,25},{9,17},{17,9},{25,1},{2,26},{10... | collective-permute-start | bytes 1572872 | tf_op jit(solution)/shard_map/ppermute | solution.py:235
  534.7 54.8 %collective-permute-start.74 = (bf16[256,4096]{1,0:T(8,128)(2,1)S(1)}, bf16[256,4096]{1,0:T(8,128)(2,1)S(1)}, u32[]{:S(2)}, u32[]{:S(2)}) collective-permute-start(bf16[256,4096]{1,0:T(8,128)(2,1)S(1)} %constant_dynamic-update-slice_fusion.6), channel_id=1, source_target_pairs={{0,2},{6,4},{1,3},{7,5},{8,10},{14,12},{9,11},{15,13},{16,18},{22,... | collective-permute-start | bytes 6291464 | tf_op jit(solution)/shard_map/ppermute | solution.py:235
  552.5 74.7 %collective-permute-start.90 = (bf16[256,4096]{1,0:T(8,128)(2,1)S(1)}, bf16[256,4096]{1,0:T(8,128)(2,1)S(1)}, u32[]{:S(2)}, u32[]{:S(2)}) collective-permute-start(bf16[256,4096]{1,0:T(8,128)(2,1)S(1)} %constant_dynamic-update-slice_fusion), channel_id=1, source_target_pairs={{0,2},{6,4},{1,3},{7,5},{8,10},{14,12},{9,11},{15,13},{16,18},{22,... | collective-permute-start | bytes 6291464 | tf_op jit(solution)/shard_map/ppermute | solution.py:235
  558.2 106.8 %collective-permute-start.101 = (bf16[4,512,512]{2,1,0:T(8,128)(2,1)S(1)}, bf16[4,512,512]{2,1,0:T(8,128)(2,1)S(1)}, u32[]{:S(2)}, u32[]{:S(2)}) collective-permute-start(bf16[4,512,512]{2,1,0:T(8,128)(2,1)S(1)} %add_convert_fusion), channel_id=1, source_target_pairs={{2,0},{4,6},{3,1},{5,7},{10,8},{12,14},{11,9},{13,15},{18,16},{20,... | collective-permute-start | bytes 6291464 | tf_op jit(solution)/shard_map/ppermute | solution.py:235
  560.3 105.0 %collective-permute-start.97 = (bf16[4,512,512]{2,1,0:T(8,128)(2,1)S(1)}, bf16[4,512,512]{2,1,0:T(8,128)(2,1)S(1)}, u32[]{:S(2)}, u32[]{:S(2)}) collective-permute-start(bf16[4,512,512]{2,1,0:T(8,128)(2,1)S(1)} %add_convert_fusion.3), channel_id=1, source_target_pairs={{2,0},{4,6},{3,1},{5,7},{10,8},{12,14},{11,9},{13,15},{18,16},{20,... | collective-permute-start | bytes 6291464 | tf_op jit(solution)/shard_map/ppermute | solution.py:235
  591.7 79.1 %collective-permute-start.47 = (bf16[512,2048]{1,0:T(8,128)(2,1)S(1)}, bf16[512,2048]{1,0:T(8,128)(2,1)S(1)}, u32[]{:S(2)}, u32[]{:S(2)}) collective-permute-start(bf16[512,2048]{1,0:T(8,128)(2,1)S(1)} %pad_maximum_fusion.8), channel_id=1, source_target_pairs={{0,8},{8,0},{16,24},{24,16},{1,9},{9,1},{17,25},{25,17},{2,10},{10... | collective-permute-start | bytes 6291464 | tf_op jit(solution)/shard_map/ppermute | solution.py:235
  629.3 155.4 %collective-permute-start.79 = (bf16[256,4096]{1,0:T(8,128)(2,1)}, bf16[256,4096]{1,0:T(8,128)(2,1)}, u32[]{:S(2)}, u32[]{:S(2)}) collective-permute-start(bf16[256,4096]{1,0:T(8,128)(2,1)} %add_convert_fusion.10), channel_id=1, source_target_pairs={{2,4},{4,2},{3,5},{5,3},{10,12},{12,10},{11,13},{13,11},{18,20},{2... | collective-permute-start | bytes 6291464 | tf_op jit(solution)/shard_map/ppermute | solution.py:235
  641.2 149.6 %collective-permute-start.75 = (bf16[256,4096]{1,0:T(8,128)(2,1)}, bf16[256,4096]{1,0:T(8,128)(2,1)}, u32[]{:S(2)}, u32[]{:S(2)}) collective-permute-start(bf16[256,4096]{1,0:T(8,128)(2,1)} %constant_dynamic-update-slice_fusion.9), channel_id=1, source_target_pairs={{0,2},{6,4},{1,3},{7,5},{8,10},{14,12},{9,11},{15,13},{16,18},{22,... | collective-permute-start | bytes 6291464 | tf_op jit(solution)/shard_map/ppermute | solution.py:235
  743.4 75.8 %collective-permute-start.94 = (bf16[256,4096]{1,0:T(8,128)(2,1)}, bf16[256,4096]{1,0:T(8,128)(2,1)}, u32[]{:S(2)}, u32[]{:S(2)}) collective-permute-start(bf16[256,4096]{1,0:T(8,128)(2,1)} %add_convert_fusion.7), channel_id=1, source_target_pairs={{2,4},{4,2},{3,5},{5,3},{10,12},{12,10},{11,13},{13,11},{18,20},{2... | collective-permute-start | bytes 6291464 | tf_op jit(solution)/shard_map/ppermute | solution.py:235
  745.4 77.6 %collective-permute-start.91 = (bf16[256,4096]{1,0:T(8,128)(2,1)}, bf16[256,4096]{1,0:T(8,128)(2,1)}, u32[]{:S(2)}, u32[]{:S(2)}) collective-permute-start(bf16[256,4096]{1,0:T(8,128)(2,1)} %constant_dynamic-update-slice_fusion.3), channel_id=1, source_target_pairs={{0,2},{6,4},{1,3},{7,5},{8,10},{14,12},{9,11},{15,13},{16,18},{22,... | collective-permute-start | bytes 6291464 | tf_op jit(solution)/shard_map/ppermute | solution.py:235
  781.0 70.0 %collective-permute-start.50 = (bf16[512,2048]{1,0:T(8,128)(2,1)}, bf16[512,2048]{1,0:T(8,128)(2,1)}, u32[]{:S(2)}, u32[]{:S(2)}) collective-permute-start(bf16[512,2048]{1,0:T(8,128)(2,1)} %convolution_convert_fusion.6), channel_id=1, source_target_pairs={{0,8},{8,0},{16,24},{24,16},{1,9},{9,1},{17,25},{25,17},{2,10},{10... | collective-permute-start | bytes 6291464 | tf_op jit(solution)/shard_map/ppermute | solution.py:235
  795.1 73.5 %collective-permute-start.102 = (bf16[256,4096]{1,0:T(8,128)(2,1)}, bf16[256,4096]{1,0:T(8,128)(2,1)}, u32[]{:S(2)}, u32[]{:S(2)}) collective-permute-start(bf16[256,4096]{1,0:T(8,128)(2,1)} %add_convert_fusion.1), channel_id=1, source_target_pairs={{2,0},{4,6},{3,1},{5,7},{10,8},{12,14},{11,9},{13,15},{18,16},{20,... | collective-permute-start | bytes 6291464 | tf_op jit(solution)/shard_map/ppermute | solution.py:235
  819.2 51.5 %collective-permute-start.80 = (bf16[256,4096]{1,0:T(8,128)(2,1)}, bf16[256,4096]{1,0:T(8,128)(2,1)S(1)}, u32[]{:S(2)}, u32[]{:S(2)}) collective-permute-start(bf16[256,4096]{1,0:T(8,128)(2,1)} %add_convert_fusion.11), channel_id=1, source_target_pairs={{2,4},{4,2},{3,5},{5,3},{10,12},{12,10},{11,13},{13,11},{18,20},{2... | collective-permute-start | bytes 6291464 | tf_op jit(solution)/shard_map/ppermute | solution.py:235
  830.3 60.4 %collective-permute-start.98 = (bf16[256,4096]{1,0:T(8,128)(2,1)S(1)}, bf16[256,4096]{1,0:T(8,128)(2,1)S(1)}, u32[]{:S(2)}, u32[]{:S(2)}) collective-permute-start(bf16[256,4096]{1,0:T(8,128)(2,1)S(1)} %add_convert_fusion.4), channel_id=1, source_target_pairs={{2,0},{4,6},{3,1},{5,7},{10,8},{12,14},{11,9},{13,15},{18,16},{20,... | collective-permute-start | bytes 6291464 | tf_op jit(solution)/shard_map/ppermute | solution.py:235
  872.2 136.8 %collective-permute-start.103 = (bf16[256,4096]{1,0:T(8,128)(2,1)S(1)}, bf16[256,4096]{1,0:T(8,128)(2,1)S(1)}, u32[]{:S(2)}, u32[]{:S(2)}) collective-permute-start(bf16[256,4096]{1,0:T(8,128)(2,1)S(1)} %add_convert_fusion.2), channel_id=1, source_target_pairs={{2,0},{4,6},{3,1},{5,7},{10,8},{12,14},{11,9},{13,15},{18,16},{20,... | collective-permute-start | bytes 6291464 | tf_op jit(solution)/shard_map/ppermute | solution.py:235
  924.6 85.9 %collective-permute-start.99 = (bf16[256,4096]{1,0:T(8,128)(2,1)S(1)}, bf16[256,4096]{1,0:T(8,128)(2,1)S(1)}, u32[]{:S(2)}, u32[]{:S(2)}) collective-permute-start(bf16[256,4096]{1,0:T(8,128)(2,1)S(1)} %add_convert_fusion.5), channel_id=1, source_target_pairs={{2,0},{4,6},{3,1},{5,7},{10,8},{12,14},{11,9},{13,15},{18,16},{20,... | collective-permute-start | bytes 6291464 | tf_op jit(solution)/shard_map/ppermute | solution.py:235
  925.9 90.7 %collective-permute-start.63 = (bf16[256,2048]{1,0:T(8,128)(2,1)S(1)}, bf16[256,2048]{1,0:T(8,128)(2,1)S(1)}, u32[]{:S(2)}, u32[]{:S(2)}) collective-permute-start(bf16[256,2048]{1,0:T(8,128)(2,1)S(1)} %fusion.14), channel_id=1, source_target_pairs={{0,1},{1,0},{2,3},{3,2},{4,5},{5,4},{6,7},{7,6},{8,9},{9,8},{10,11... | collective-permute-start | bytes 3145736 | tf_op jit(solution)/shard_map/ppermute | solution.py:235
  926.5 77.4 %collective-permute-start.83 = (f32[2,512]{1,0:T(2,128)S(1)}, f32[2,512]{1,0:T(2,128)S(1)}, u32[]{:S(2)}, u32[]{:S(2)}) collective-permute-start(f32[2,512]{1,0:T(2,128)S(1)} %add_add_fusion), channel_id=1, source_target_pairs={{0,2},{2,0},{4,6},{6,4},{1,3},{3,1},{5,7},{7,5},{8,10},{10,8},{12,... | collective-permute-start | bytes 12296 | tf_op jit(solution)/shard_map/ppermute | solution.py:505
  (140 other events, 2976.8 us)
